TPU v7x, 256 devices: a whole 4x4x8 slice. The times are simulated.
256 devices in a mesh: section: 32 (over y, x, z_lo), tensor: 8 (over z_hi, core).
Axes of the slice: x: 4, y: 4, z: 8 (z_hi: 4, z_lo: 2; z = z_hi * 2 + z_lo), core: 2. Of those that a mesh axis runs over, the one named last changes fastest.
Arguments:
- embedded: bfloat16 [256, 4096], P(None, 'tensor'), may hold values from -6 to 6
- outbox: bfloat16 [32, 256, 4096], P('section', None, 'tensor'), may hold values from -6 to 6
- loss_grad: bfloat16 [256, 4096], P(None, 'tensor'), may hold values from -6 to 6
- grad_outbox: bfloat16 [32, 256, 4096], P('section', None, 'tensor'), may hold values from -6 to 6
- stash_held: bfloat16 [32, 256, 4096], P('section', None, 'tensor'), may hold values from -6 to 6
- norm_gain: bfloat16 [32, 4096], P('section', 'tensor'), may hold values from 0.099609375 to 1.8984375
- w_query: bfloat16 [32, 4096, 4096], P('section', None, 'tensor'), may hold values from -4 to 4
- w_keyval: bfloat16 [32, 4096, 2048], P('section', None, 'tensor'), may hold values from -1 to 1
- w_out: bfloat16 [32, 4096, 4096], P('section', 'tensor'), may hold values from -0.125 to 0.125
Outputs:
- section_out: bfloat16 [32, 256, 4096], P('section', None, 'tensor')
- evicted: bfloat16 [32, 256, 4096], P('section', None, 'tensor')
- input_grad: bfloat16 [32, 256, 4096], P('section', None, 'tensor')
All inputs are finite; a program needn't handle non-finite values.
Results may differ from a plain program's by a relative error of at most 0.013.
Values may be sent and summed in bfloat16 or wider, within the bound.
A program may use at most 64 MiB of HBM per device.

v0:
```python
import jax
import jax.numpy as jnp
from jax import lax
from jax.sharding import PartitionSpec as P

D = 4096
HEAD = 128


EPS = 1e-05


def from_partner(block, axis, bit):
    count = lax.axis_size(axis)
    route = []
    for low in range(count):
        high = low | 1 << bit
        if high != low and high < count:
            route += [(low, high), (high, low)]
    return lax.ppermute(block, axis, route)


def shifted(value, axis, steps):
    count = lax.axis_size(axis)
    first, last = (max(0, -steps), min(count, count - steps))
    return lax.ppermute(value, axis, [(source, source + steps) for source in range(first, last)])


def normalize_project(x_full, gain_full, w_query, w_keyval):
    xf = x_full.astype(jnp.float32)
    inv = lax.rsqrt(jnp.mean(xf * xf, axis=-1, keepdims=True) + EPS)
    normed = (xf * inv * gain_full.astype(jnp.float32)).astype(jnp.bfloat16)
    query = jnp.dot(normed, w_query, preferred_element_type=jnp.float32).astype(jnp.bfloat16)
    keyval = jnp.dot(normed, w_keyval, preferred_element_type=jnp.float32).astype(jnp.bfloat16)
    return (inv, query, keyval)


def attend_local(query, keyval, heads):
    seq = query.shape[0]
    split = query.reshape(seq, heads, HEAD)
    keys = keyval[:, :HEAD]
    values = keyval[:, HEAD:]
    scores = jnp.einsum("shd,td->hst", split, keys, preferred_element_type=jnp.float32) * HEAD ** (
        -0.5
    )
    rows = lax.broadcasted_iota(jnp.int32, (seq, seq), 0)
    cols = lax.broadcasted_iota(jnp.int32, (seq, seq), 1)
    scores = jnp.where(rows >= cols, scores, -1e30)
    top = jnp.max(scores, axis=-1, keepdims=True)
    weights = jnp.exp(scores - top)
    prob = weights / jnp.sum(weights, axis=-1, keepdims=True)
    prob_low = prob.astype(jnp.bfloat16)
    attn = jnp.einsum("hst,td->shd", prob_low, values, preferred_element_type=jnp.float32)
    return (
        prob,
        prob_low,
        split,
        keys,
        values,
        attn.astype(jnp.bfloat16).reshape(seq, heads * HEAD),
    )


def send_to_pair(value, bits):
    for bit_number in range(bits):
        value = from_partner(value, "section", bit_number)
    return value


def fetch_shard_back(value, bits):
    order = range(bits)
    for bit_number in order:
        value = from_partner(value, "section", bit_number)
    return value


def local(
    embedded, outbox, loss_grad, grad_outbox, stash_held, norm_gain, w_query, w_keyval, w_out
):
    sections = lax.axis_size("section")
    position = lax.axis_index("section")
    bits = sections.bit_length() - 1
    column = lax.axis_index("tensor")
    width = outbox.shape[2]
    wq = w_query[0]
    wkv = w_keyval[0]
    wo = w_out[0]
    heads = wq.shape[1] // HEAD
    arrived = shifted(outbox[0], "section", 1)
    x_shard = jnp.where(position == 0, embedded, arrived)
    coming = shifted(grad_outbox[0], "section", -1)
    grad_shard = jnp.where(position == sections - 1, loss_grad, coming)
    evicted = send_to_pair(x_shard, bits)
    x_full, gain_full = (
        lax.all_gather(x_shard, "tensor", axis=1, tiled=True),
        lax.all_gather(norm_gain, "tensor", axis=1, tiled=True),
    )
    inv, query, keyval = normalize_project(x_full, gain_full, wq, wkv)
    attn = attend_local(query, keyval, heads)[5]
    partial_value = jnp.dot(attn, wo, preferred_element_type=jnp.float32)
    mixed = lax.psum_scatter(
        partial_value.astype(jnp.bfloat16), "tensor", scatter_dimension=1, tiled=True
    ).astype(jnp.float32)
    section_out = (x_shard.astype(jnp.float32) + mixed).astype(jnp.bfloat16)
    fetched = fetch_shard_back(stash_held[0], bits)
    stash_full, grad_full = (
        lax.all_gather(fetched, "tensor", axis=1, tiled=True),
        lax.all_gather(grad_shard, "tensor", axis=1, tiled=True),
    )
    stash_shard = lax.dynamic_slice_in_dim(stash_full, column * width, width, 1)
    inv_back, query_back, keyval_back = normalize_project(stash_full, gain_full, wq, wkv)
    prob, prob_low, split, keys, values, unused = attend_local(query_back, keyval_back, heads)
    seq = stash_full.shape[0]
    d_attn = lax.dot_general(
        grad_full, wo, (((1,), (1,)), ((), ())), preferred_element_type=jnp.float32
    ).astype(jnp.bfloat16)
    d_heads = d_attn.reshape(seq, heads, HEAD)
    d_prob = jnp.einsum("shd,td->hst", d_heads, values, preferred_element_type=jnp.float32)
    d_score = prob * (d_prob - jnp.sum(prob * d_prob, axis=-1, keepdims=True)) * HEAD ** (-0.5)
    d_score = d_score.astype(jnp.bfloat16)
    d_query = jnp.einsum("hst,td->shd", d_score, keys, preferred_element_type=jnp.float32)
    d_query = d_query.astype(jnp.bfloat16).reshape(seq, heads * HEAD)
    d_key = jnp.einsum("hst,shd->td", d_score, split, preferred_element_type=jnp.float32).astype(
        jnp.bfloat16
    )
    d_value = jnp.einsum(
        "hst,shd->td", prob_low, d_heads, preferred_element_type=jnp.float32
    ).astype(jnp.bfloat16)
    d_pairs = jnp.concatenate([d_key, d_value], axis=1)
    back_terms = lax.dot_general(
        d_query, wq, (((1,), (1,)), ((), ())), preferred_element_type=jnp.float32
    )
    back_terms = back_terms + lax.dot_general(
        d_pairs, wkv, (((1,), (1,)), ((), ())), preferred_element_type=jnp.float32
    )
    summed = lax.psum(back_terms.astype(jnp.bfloat16), "tensor").astype(jnp.float32)
    scaled_full = summed * gain_full.astype(jnp.float32)
    total = jnp.sum(scaled_full * stash_full.astype(jnp.float32), axis=-1, keepdims=True)
    scaled = lax.dynamic_slice_in_dim(scaled_full, column * width, width, 1)
    correction = total / D
    stash_float = stash_shard.astype(jnp.float32)
    result = (
        grad_shard.astype(jnp.float32) + inv_back * scaled - stash_float * inv_back**3 * correction
    )
    return (section_out[None], evicted[None], result.astype(jnp.bfloat16)[None])


def solution(mesh):
    return jax.shard_map(
        local,
        mesh=mesh,
        in_specs=(
            P(None, "tensor"),
            P("section", None, "tensor"),
            P(None, "tensor"),
            P("section", None, "tensor"),
            P("section", None, "tensor"),
            P("section", "tensor"),
            P("section", None, "tensor"),
            P("section", None, "tensor"),
            P("section", "tensor", None),
        ),
        out_specs=(
            P("section", None, "tensor"),
            P("section", None, "tensor"),
            P("section", None, "tensor"),
        ),
        check_vma=False,
    )
```

profile of v0, /device:TPU:33, one launch (start us, length us, event | category | flops | bytes accessed | tf_op | source)
XLA Modules:
  0.0 296.7 jit_solution(1310918328935990307)
XLA Ops:
  7.2 0.0 all-gather.4.cloned.1.call-start
  7.2 2.8 collective-permute-start
  10.0 6.6 %collective-permute-done = bf16[256,512]{1,0:T(8,128)(2,1)S(1)} collective-permute-done((bf16[256,512]{1,0:T(8,128)(2,1)}, bf16[256,512]{1,0:T(8,128)(2,1)S(1)}, u32[]{:S(2)}, u32[]{:S(2)}) %collective-permute-start) | collective-permute-done | bytes 262176 | tf_op jit(solution)/shard_map/ppermute | solution.py:26
  16.6 0.7 broadcast_select_fusion.1
  17.4 0.0 all-gather.8.cloned.1.call-start
  17.4 2.2 collective-permute-start.6
  19.7 7.0 %collective-permute-done.6 = bf16[256,512]{1,0:T(8,128)(2,1)S(1)} collective-permute-done((bf16[256,512]{1,0:T(8,128)(2,1)}, bf16[256,512]{1,0:T(8,128)(2,1)S(1)}, u32[]{:S(2)}, u32[]{:S(2)}) %collective-permute-start.6) | collective-permute-done | bytes 262176 | tf_op jit(solution)/shard_map/ppermute | solution.py:26
  26.7 0.7 broadcast_select_fusion
  27.5 0.0 all-gather.6.cloned.1.call-start
  27.5 0.1 collective-permute-start.7
  27.6 5.4 %collective-permute-done.7 = bf16[256,512]{1,0:T(8,128)(2,1)S(1)} collective-permute-done((bf16[256,512]{1,0:T(8,128)(2,1)}, bf16[256,512]{1,0:T(8,128)(2,1)S(1)}, u32[]{:S(2)}, u32[]{:S(2)}) %collective-permute-start.7) | collective-permute-done | bytes 262176 | tf_op jit(solution)/shard_map/ppermute | solution.py:20
  33.0 1.2 collective-permute-start.8
  34.2 4.0 %collective-permute-done.8 = bf16[256,512]{1,0:T(8,128)(2,1)S(1)} collective-permute-done((bf16[256,512]{1,0:T(8,128)(2,1)S(1)}, bf16[256,512]{1,0:T(8,128)(2,1)S(1)}, u32[]{:S(2)}, u32[]{:S(2)}) %collective-permute-start.8) | collective-permute-done | bytes 262176 | tf_op jit(solution)/shard_map/ppermute | solution.py:20
  38.3 4.7 %collective-permute-start.9 = (bf16[256,512]{1,0:T(8,128)(2,1)S(1)}, bf16[256,512]{1,0:T(8,128)(2,1)S(1)}, u32[]{:S(2)}, u32[]{:S(2)}) collective-permute-start(bf16[256,512]{1,0:T(8,128)(2,1)S(1)} %collective-permute-done.8), channel_id=1, source_target_pairs={{0,32},{32,0},{8,40},{40,8},{16,48},{48,16},{24,56},{56,24},{64,96... | collective-permute-start | bytes 786440 | tf_op jit(solution)/shard_map/ppermute | solution.py:20
  43.0 4.2 %collective-permute-done.9 = bf16[256,512]{1,0:T(8,128)(2,1)S(1)} collective-permute-done((bf16[256,512]{1,0:T(8,128)(2,1)S(1)}, bf16[256,512]{1,0:T(8,128)(2,1)S(1)}, u32[]{:S(2)}, u32[]{:S(2)}) %collective-permute-start.9) | collective-permute-done | bytes 262176 | tf_op jit(solution)/shard_map/ppermute | solution.py:20
  47.1 1.0 collective-permute-start.10
  48.1 4.6 %collective-permute-done.10 = bf16[256,512]{1,0:T(8,128)(2,1)S(1)} collective-permute-done((bf16[256,512]{1,0:T(8,128)(2,1)S(1)}, bf16[256,512]{1,0:T(8,128)(2,1)S(1)}, u32[]{:S(2)}, u32[]{:S(2)}) %collective-permute-start.10) | collective-permute-done | bytes 262176 | tf_op jit(solution)/shard_map/ppermute | solution.py:20
  52.7 3.1 %collective-permute-start.11 = (bf16[256,512]{1,0:T(8,128)(2,1)S(1)}, bf16[256,512]{1,0:T(8,128)(2,1)S(1)}, u32[]{:S(2)}, u32[]{:S(2)}) collective-permute-start(bf16[256,512]{1,0:T(8,128)(2,1)S(1)} %collective-permute-done.10), channel_id=1, source_target_pairs={{0,128},{128,0},{8,136},{136,8},{16,144},{144,16},{24,152},{152,24... | collective-permute-start | bytes 786440 | tf_op jit(solution)/shard_map/ppermute | solution.py:20
  55.8 3.8 %collective-permute-done.11 = bf16[256,512]{1,0:T(8,128)(2,1)S(1)} collective-permute-done((bf16[256,512]{1,0:T(8,128)(2,1)S(1)}, bf16[256,512]{1,0:T(8,128)(2,1)S(1)}, u32[]{:S(2)}, u32[]{:S(2)}) %collective-permute-start.11) | collective-permute-done | bytes 262176 | tf_op jit(solution)/shard_map/ppermute | solution.py:20
  59.6 0.7 copy-done.7
  60.3 0.0 all-reduce.2.cloned.1.call-start
  60.4 37.7 %all_gather.13 = bf16[1,4096]{1,0:T(2,128)(2,1)S(1)} all-gather(bf16[1,512]{1,0:T(2,128)(2,1)} %param.14), channel_id=1, replica_groups=mesh['section'=32,'tensor'=8] {'tensor'}, dimensions={1}, use_global_device_ids=true | all-gather | bytes 9216 | tf_op jit(solution)/shard_map/all_gather | solution.py:96
  98.1 0.0 all-gather.4.cloned.1.call-done
  98.2 2.7 fusion.4
  100.8 4.1 %fusion.46 = bf16[32,4,8,128]{3,2,1,0:T(8,128)(2,1)S(1)} fusion(bf16[256,4096]{1,0:T(8,128)(2,1)} %all-gather.8.cloned.1.call-done, bf16[1,512,4096]{2,1,0:T(8,128)(2,1)} %param.17), kind=kOutput, calls=%fused_computation.53 | convolution fusion | flops 1073872896 | bytes 6553600 | tf_op jit(solution)/shard_map/dot_general | solution.py:114
  104.9 30.6 %all-gather.6.cloned.1.call-done = bf16[256,4096]{1,0:T(8,128)(2,1)} async-done(((bf16[256,512]{1,0:T(8,128)(2,1)}), bf16[256,4096]{1,0:T(8,128)(2,1)}) %all-gather.6.cloned.1.call-update) | async-done | bytes 2097168 | tf_op jit(solution)/shard_map/all_gather | solution.py:107
  135.5 2.1 fusion.7
  137.6 0.5 multiply_multiply_fusion
  138.2 2.6 fusion.58
  140.8 0.6 copy-done.10
  141.4 0.3 convolution_bitcast_fusion
  141.8 2.0 fusion.49
  143.8 2.4 fusion.113
  146.2 0.6 copy-done.16
  146.7 2.0 fusion.61
  148.8 2.0 convolution_convert_fusion.1
  150.8 1.8 fusion.62
  152.6 3.5 %fusion.14 = f32[256,4096]{1,0:T(8,128)S(1)} fusion(bf16[256,512]{0,1:T(8,128)(2,1)S(1)} %bitcast.147, bf16[1,4096,512]{2,1,0:T(8,128)(2,1)} %param.15), kind=kOutput, calls=%fused_computation.21 | convolution fusion | flops 1073741824 | bytes 8650752 | tf_op jit(solution)/shard_map/dot_general | solution.py:130
  156.1 2.1 fusion.3
  158.2 0.2 reduce-scatter.2.cloned.1.call-start
  158.5 2.5 fusion.55
  161.0 0.3 copy-done.3
  161.3 0.7 copy-done.6
  162.0 1.3 fusion.52
  163.3 0.5 fusion.110
  163.8 1.1 fusion.35
  164.9 1.2 convolution_convert_fusion.2
  166.2 4.8 %convolution_convert_fusion = bf16[256,4096]{1,0:T(8,128)(2,1)} fusion(bf16[256,512]{0,1:T(8,128)(2,1)S(1)} %bitcast.148, bf16[1,512,4096]{2,1,0:T(8,128)(2,1)} %param.17), kind=kOutput, calls=%fused_computation.10 | convolution fusion | flops 1074790400 | bytes 6553600 | tf_op jit(solution)/shard_map/dot_general | solution.py:100
  171.1 1.5 collective-permute-start.1
  172.6 12.6 %collective-permute-done.1 = bf16[256,512]{1,0:T(8,128)(2,1)S(1)} collective-permute-done((bf16[256,512]{1,0:T(8,128)(2,1)S(1)}, bf16[256,512]{1,0:T(8,128)(2,1)S(1)}, u32[]{:S(2)}, u32[]{:S(2)}) %collective-permute-start.1) | collective-permute-done | bytes 262176 | tf_op jit(solution)/shard_map/ppermute | solution.py:20
  185.1 1.2 collective-permute-start.2
  186.3 5.6 %collective-permute-done.2 = bf16[256,512]{1,0:T(8,128)(2,1)S(1)} collective-permute-done((bf16[256,512]{1,0:T(8,128)(2,1)S(1)}, bf16[256,512]{1,0:T(8,128)(2,1)S(1)}, u32[]{:S(2)}, u32[]{:S(2)}) %collective-permute-start.2) | collective-permute-done | bytes 262176 | tf_op jit(solution)/shard_map/ppermute | solution.py:20
  191.9 2.7 collective-permute-start.3
  194.6 4.7 %collective-permute-done.3 = bf16[256,512]{1,0:T(8,128)(2,1)S(1)} collective-permute-done((bf16[256,512]{1,0:T(8,128)(2,1)S(1)}, bf16[256,512]{1,0:T(8,128)(2,1)S(1)}, u32[]{:S(2)}, u32[]{:S(2)}) %collective-permute-start.3) | collective-permute-done | bytes 262176 | tf_op jit(solution)/shard_map/ppermute | solution.py:20
  199.4 1.4 collective-permute-start.4
  200.7 3.9 %collective-permute-done.4 = bf16[256,512]{1,0:T(8,128)(2,1)S(1)} collective-permute-done((bf16[256,512]{1,0:T(8,128)(2,1)S(1)}, bf16[256,512]{1,0:T(8,128)(2,1)S(1)}, u32[]{:S(2)}, u32[]{:S(2)}) %collective-permute-start.4) | collective-permute-done | bytes 262176 | tf_op jit(solution)/shard_map/ppermute | solution.py:20
  204.6 2.9 collective-permute-start.5
  207.5 5.3 %collective-permute-done.5 = bf16[256,512]{1,0:T(8,128)(2,1)S(1)} collective-permute-done((bf16[256,512]{1,0:T(8,128)(2,1)S(1)}, bf16[256,512]{1,0:T(8,128)(2,1)S(1)}, u32[]{:S(2)}, u32[]{:S(2)}) %collective-permute-start.5) | collective-permute-done | bytes 262176 | tf_op jit(solution)/shard_map/ppermute | solution.py:20
  212.8 31.0 %all-reduce.2.cloned.1.call-done = bf16[256,4096]{1,0:T(8,128)(2,1)} async-done(((bf16[256,4096]{1,0:T(8,128)(2,1)}), bf16[256,4096]{1,0:T(8,128)(2,1)}) %all-reduce.2.cloned.1.call-update) | async-done | bytes 2097168 | tf_op jit(solution)/shard_map/psum | solution.py:136
  243.8 3.0 %fusion.10 = (f32[256]{0:T(256)S(1)}, f32[256,4096]{1,0:T(8,128)S(1)}) fusion(bf16[256,4096]{1,0:T(8,128)(2,1)} %all-gather.6.cloned.1.call-done, f32[4096]{0:T(1024)S(1)} %bitcast.154, bf16[256,4096]{1,0:T(8,128)(2,1)} %all-reduce.2.cloned.1.call-done), kind=kLoop, calls=%fused_computation.17 | loop fusion | flops 5242624 | bytes 8406016 | tf_op jit(solution)/shard_map/reduce_sum | solution.py:138
  246.8 1.9 fusion.75
  248.7 39.0 %reduce-scatter.2.cloned.1.call-done = bf16[256,512]{1,0:T(8,128)(2,1)} async-done(((bf16[256,4096]{1,0:T(8,128)(2,1)}), bf16[256,512]{1,0:T(8,128)(2,1)}) %reduce-scatter.2.cloned.1.call-update) | async-done | bytes 262160 | tf_op jit(solution)/shard_map/reduce_scatter | solution.py:101
  287.7 1.7 fusion.74
  289.4 0.7 copy.64
  (39 shorter events, 0.2 us)
Async XLA Ops:
  7.2 131.0 %copy-start = (bf16[1,4096,256]{2,1,0:T(8,128)(2,1)S(1)}, bf16[1,4096,256]{2,1,0:T(8,128)(2,1)}, u32[]{:S(2)}) copy-start(bf16[1,4096,256]{2,1,0:T(8,128)(2,1)} %param.16) | copy-start | bytes 6291460
  7.2 91.0 %all-gather.4.cloned.1.call-start = ((), (), s32[]{:S(2)}) async-start(), calls=%async_computation.1 | async-start | bytes 2359296 | tf_op jit(solution)/shard_map/all_gather | solution.py:95
  7.2 9.4 %collective-permute-start = (bf16[256,512]{1,0:T(8,128)(2,1)}, bf16[256,512]{1,0:T(8,128)(2,1)S(1)}, u32[]{:S(2)}, u32[]{:S(2)}) collective-permute-start(bf16[256,512]{1,0:T(8,128)(2,1)} %bitcast.155), channel_id=1, source_target_pairs={{0,8},{8,16},{16,24},{24,32},{32,40},{40,48},{48,56},{56,64},{64,7... | collective-permute-start | bytes 786440 | tf_op jit(solution)/shard_map/ppermute | solution.py:26
  17.4 83.4 %all-gather.8.cloned.1.call-start = ((), (), s32[]{:S(2)}) async-start(), calls=%async_computation.4 | async-start | bytes 2359296 | tf_op jit(solution)/shard_map/all_gather | solution.py:108
  17.4 9.3 %collective-permute-start.6 = (bf16[256,512]{1,0:T(8,128)(2,1)}, bf16[256,512]{1,0:T(8,128)(2,1)S(1)}, u32[]{:S(2)}, u32[]{:S(2)}) collective-permute-start(bf16[256,512]{1,0:T(8,128)(2,1)} %bitcast.156), channel_id=1, source_target_pairs={{8,0},{16,8},{24,16},{32,24},{40,32},{48,40},{56,48},{64,56},{72,6... | collective-permute-start | bytes 786440 | tf_op jit(solution)/shard_map/ppermute | solution.py:26
  27.5 108.0 %all-gather.6.cloned.1.call-start = ((), (), s32[]{:S(2)}) async-start(), calls=%async_computation.3 | async-start | bytes 2359296 | tf_op jit(solution)/shard_map/all_gather | solution.py:107
  27.5 5.5 %collective-permute-start.7 = (bf16[256,512]{1,0:T(8,128)(2,1)}, bf16[256,512]{1,0:T(8,128)(2,1)S(1)}, u32[]{:S(2)}, u32[]{:S(2)}) collective-permute-start(bf16[256,512]{1,0:T(8,128)(2,1)} %bitcast.157), channel_id=1, source_target_pairs={{0,8},{8,0},{16,24},{24,16},{32,40},{40,32},{48,56},{56,48},{64,72... | collective-permute-start | bytes 786440 | tf_op jit(solution)/shard_map/ppermute | solution.py:20
  33.0 5.2 %collective-permute-start.8 = (bf16[256,512]{1,0:T(8,128)(2,1)S(1)}, bf16[256,512]{1,0:T(8,128)(2,1)S(1)}, u32[]{:S(2)}, u32[]{:S(2)}) collective-permute-start(bf16[256,512]{1,0:T(8,128)(2,1)S(1)} %collective-permute-done.7), channel_id=1, source_target_pairs={{0,16},{16,0},{8,24},{24,8},{32,48},{48,32},{40,56},{56,40},{64,80... | collective-permute-start | bytes 786440 | tf_op jit(solution)/shard_map/ppermute | solution.py:20
  38.3 8.9 %collective-permute-start.9 = (bf16[256,512]{1,0:T(8,128)(2,1)S(1)}, bf16[256,512]{1,0:T(8,128)(2,1)S(1)}, u32[]{:S(2)}, u32[]{:S(2)}) collective-permute-start(bf16[256,512]{1,0:T(8,128)(2,1)S(1)} %collective-permute-done.8), channel_id=1, source_target_pairs={{0,32},{32,0},{8,40},{40,8},{16,48},{48,16},{24,56},{56,24},{64,96... | collective-permute-start | bytes 786440 | tf_op jit(solution)/shard_map/ppermute | solution.py:20
  47.1 5.6 %collective-permute-start.10 = (bf16[256,512]{1,0:T(8,128)(2,1)S(1)}, bf16[256,512]{1,0:T(8,128)(2,1)S(1)}, u32[]{:S(2)}, u32[]{:S(2)}) collective-permute-start(bf16[256,512]{1,0:T(8,128)(2,1)S(1)} %collective-permute-done.9), channel_id=1, source_target_pairs={{0,64},{64,0},{8,72},{72,8},{16,80},{80,16},{24,88},{88,24},{32,96... | collective-permute-start | bytes 786440 | tf_op jit(solution)/shard_map/ppermute | solution.py:20
  52.7 6.8 %collective-permute-start.11 = (bf16[256,512]{1,0:T(8,128)(2,1)S(1)}, bf16[256,512]{1,0:T(8,128)(2,1)S(1)}, u32[]{:S(2)}, u32[]{:S(2)}) collective-permute-start(bf16[256,512]{1,0:T(8,128)(2,1)S(1)} %collective-permute-done.10), channel_id=1, source_target_pairs={{0,128},{128,0},{8,136},{136,8},{16,144},{144,16},{24,152},{152,24... | collective-permute-start | bytes 786440 | tf_op jit(solution)/shard_map/ppermute | solution.py:20
  59.6 0.7 copy-start.7
  60.3 183.5 %all-reduce.2.cloned.1.call-start = ((), (), s32[]{:S(2)}) async-start(), calls=%async_computation.5 | async-start | bytes 4194304 | tf_op jit(solution)/shard_map/psum | solution.py:136
  104.9 35.9 %copy-start.8 = (bf16[32,4,8,128]{3,2,1,0:T(8,128)(2,1)}, bf16[32,4,8,128]{3,2,1,0:T(8,128)(2,1)S(1)}, u32[]{:S(2)}) copy-start(bf16[32,4,8,128]{3,2,1,0:T(8,128)(2,1)S(1)} %fusion.46) | copy-start | bytes 786436
  137.6 4.1 %copy-start.1 = (bf16[256,4096]{1,0:T(8,128)(2,1)S(1)}, bf16[256,4096]{1,0:T(8,128)(2,1)}, u32[]{:S(2)}) copy-start(bf16[256,4096]{1,0:T(8,128)(2,1)} %all-gather.6.cloned.1.call-done) | copy-start | bytes 6291460
  137.6 4.1 %copy-start.2 = (bf16[1,4096,512]{2,1,0:T(8,128)(2,1)S(1)}, bf16[1,4096,512]{2,1,0:T(8,128)(2,1)}, u32[]{:S(2)}) copy-start(bf16[1,4096,512]{2,1,0:T(8,128)(2,1)} %param.15) | copy-start | bytes 12582916
  138.1 5.6 %copy-start.14 = (f32[256]{0:T(256)}, f32[256]{0:T(256)S(1)}, u32[]{:S(2)}) copy-start(f32[256]{0:T(256)S(1)} %get-tuple-element.6) | copy-start | bytes 3076
  140.8 0.7 copy-start.10
  141.7 2.0 copy-start.11
  146.2 0.6 copy-start.16
  156.1 2.4 copy-start.12
  158.2 129.5 %reduce-scatter.2.cloned.1.call-start = ((), (), s32[]{:S(2)}) async-start(), calls=%async_computation.2 | async-start | bytes 2359296 | tf_op jit(solution)/shard_map/reduce_scatter | solution.py:101
  158.5 2.8 copy-start.3
  158.5 3.5 %copy-start.6 = (bf16[256,4096]{1,0:T(8,128)(2,1)S(1)}, bf16[256,4096]{1,0:T(8,128)(2,1)}, u32[]{:S(2)}) copy-start(bf16[256,4096]{1,0:T(8,128)(2,1)} %all-gather.4.cloned.1.call-done) | copy-start | bytes 6291460
  162.0 1.3 copy-start.9
  166.2 4.9 %copy-start.4 = (bf16[256,512]{1,0:T(8,128)(2,1)S(1)}, bf16[256,512]{1,0:T(8,128)(2,1)}, u32[]{:S(2)}) copy-start(bf16[256,512]{1,0:T(8,128)(2,1)} %broadcast_select_fusion.1) | copy-start | bytes 786436
  171.1 14.1 %collective-permute-start.1 = (bf16[256,512]{1,0:T(8,128)(2,1)S(1)}, bf16[256,512]{1,0:T(8,128)(2,1)S(1)}, u32[]{:S(2)}, u32[]{:S(2)}) collective-permute-start(bf16[256,512]{1,0:T(8,128)(2,1)S(1)} %copy-done.4), channel_id=1, source_target_pairs={{0,8},{8,0},{16,24},{24,16},{32,40},{40,32},{48,56},{56,48},{64,72... | collective-permute-start | bytes 786440 | tf_op jit(solution)/shard_map/ppermute | solution.py:20
  185.1 6.8 %collective-permute-start.2 = (bf16[256,512]{1,0:T(8,128)(2,1)S(1)}, bf16[256,512]{1,0:T(8,128)(2,1)S(1)}, u32[]{:S(2)}, u32[]{:S(2)}) collective-permute-start(bf16[256,512]{1,0:T(8,128)(2,1)S(1)} %collective-permute-done.1), channel_id=1, source_target_pairs={{0,16},{16,0},{8,24},{24,8},{32,48},{48,32},{40,56},{56,40},{64,80... | collective-permute-start | bytes 786440 | tf_op jit(solution)/shard_map/ppermute | solution.py:20
  191.9 7.5 %collective-permute-start.3 = (bf16[256,512]{1,0:T(8,128)(2,1)S(1)}, bf16[256,512]{1,0:T(8,128)(2,1)S(1)}, u32[]{:S(2)}, u32[]{:S(2)}) collective-permute-start(bf16[256,512]{1,0:T(8,128)(2,1)S(1)} %collective-permute-done.2), channel_id=1, source_target_pairs={{0,32},{32,0},{8,40},{40,8},{16,48},{48,16},{24,56},{56,24},{64,96... | collective-permute-start | bytes 786440 | tf_op jit(solution)/shard_map/ppermute | solution.py:20
  199.4 5.2 %collective-permute-start.4 = (bf16[256,512]{1,0:T(8,128)(2,1)S(1)}, bf16[256,512]{1,0:T(8,128)(2,1)S(1)}, u32[]{:S(2)}, u32[]{:S(2)}) collective-permute-start(bf16[256,512]{1,0:T(8,128)(2,1)S(1)} %collective-permute-done.3), channel_id=1, source_target_pairs={{0,64},{64,0},{8,72},{72,8},{16,80},{80,16},{24,88},{88,24},{32,96... | collective-permute-start | bytes 786440 | tf_op jit(solution)/shard_map/ppermute | solution.py:20
  204.6 8.2 %collective-permute-start.5 = (bf16[256,512]{1,0:T(8,128)(2,1)S(1)}, bf16[256,512]{1,0:T(8,128)(2,1)S(1)}, u32[]{:S(2)}, u32[]{:S(2)}) collective-permute-start(bf16[256,512]{1,0:T(8,128)(2,1)S(1)} %collective-permute-done.4), channel_id=1, source_target_pairs={{0,128},{128,0},{8,136},{136,8},{16,144},{144,16},{24,152},{152,24... | collective-permute-start | bytes 786440 | tf_op jit(solution)/shard_map/ppermute | solution.py:20
  212.8 34.0 %copy-start.5 = (bf16[256,512]{1,0:T(8,128)(2,1)S(1)}, bf16[256,512]{1,0:T(8,128)(2,1)}, u32[]{:S(2)}) copy-start(bf16[256,512]{1,0:T(8,128)(2,1)} %broadcast_select_fusion) | copy-start | bytes 786436
  212.8 34.0 %copy-start.13 = (f32[256]{0:T(256)S(1)}, f32[256]{0:T(256)}, u32[]{:S(2)}) copy-start(f32[256]{0:T(256)} %get-tuple-element.5) | copy-start | bytes 3076
  212.8 34.0 %copy-start.15 = (f32[256]{0:T(256)S(1)}, f32[256]{0:T(256)}, u32[]{:S(2)}) copy-start(f32[256]{0:T(256)} %copy-done.14) | copy-start | bytes 3076
Sparse Core Ops, SparseCore 0:
  17.5 39.9 all-gather.3
  59.9 38.6 all-gather.7
  101.0 34.4 all-gather.5
  158.3 85.4 all-reduce.1
  246.2 41.4 reduce-scatter.1
where the time goes:
time: 301 us; the launch traced here: 297 us
  waiting for transfers between devices  168 us (56%)
  blocking collectives  37.7 us (13%)
  matrix products  34.3 us (11%)
  starting transfers between devices  25.1 us (8%)
  between operations  14.1 us (5%)
  other arithmetic  13.4 us (4%)
  local copies, waits for them, and re-layouts  3.66 us (1%)
    ppermute x10, waiting for transfers between devices, from_partner(): return lax.ppermute(block, axis, route)  54.1 us
    reduce_scatter x1, waiting for transfers between devices, local(): lax.psum_scatter(partial_value.astype(jnp.bfloat16), 'tensor', scatter_di...  39 us
    all_gather x1, blocking collectives, local(): lax.all_gather(norm_gain, 'tensor', axis=1, tiled=True)  37.7 us
    psum x1, waiting for transfers between devices, local(): lax.psum(back_terms.astype(jnp.bfloat16), 'tensor').astype(jnp.float32)  31 us
    all_gather x1, waiting for transfers between devices, local(): lax.all_gather(fetched, 'tensor', axis=1, tiled=True)  30.6 us
    ppermute x10, starting transfers between devices, from_partner(): return lax.ppermute(block, axis, route)  19.7 us
    ppermute x2, waiting for transfers between devices, shifted(): lax.ppermute(value, axis, [(source, source + steps) for source in range(f...  13.6 us
  transfers between devices with their start and end apart: 17, of which 15 were waited for; matrix products, arithmetic and copies ran while one was open for 8% of the time, Pallas kernels for 0%

commit v1 on v0

--- a/solution.py
+++ b/solution.py
@@ -10,14 +10,8 @@
 EPS = 1e-05
 
 
-def from_partner(block, axis, bit):
-    count = lax.axis_size(axis)
-    route = []
-    for low in range(count):
-        high = low | 1 << bit
-        if high != low and high < count:
-            route += [(low, high), (high, low)]
-    return lax.ppermute(block, axis, route)
+def mirrored(value, axis, last):
+    return lax.ppermute(value, axis, [(source, last - source) for source in range(last + 1)])
 
 
 def shifted(value, axis, steps):
@@ -61,27 +55,11 @@
     )
 
 
-def send_to_pair(value, bits):
-    for bit_number in range(bits):
-        value = from_partner(value, "section", bit_number)
-    return value
-
-
-def fetch_shard_back(value, bits):
-    order = range(bits)
-    for bit_number in order:
-        value = from_partner(value, "section", bit_number)
-    return value
-
-
 def local(
     embedded, outbox, loss_grad, grad_outbox, stash_held, norm_gain, w_query, w_keyval, w_out
 ):
     sections = lax.axis_size("section")
     position = lax.axis_index("section")
-    bits = sections.bit_length() - 1
-    column = lax.axis_index("tensor")
-    width = outbox.shape[2]
     wq = w_query[0]
     wkv = w_keyval[0]
     wo = w_out[0]
@@ -90,7 +68,10 @@
     x_shard = jnp.where(position == 0, embedded, arrived)
     coming = shifted(grad_outbox[0], "section", -1)
     grad_shard = jnp.where(position == sections - 1, loss_grad, coming)
-    evicted = send_to_pair(x_shard, bits)
+    evicted = jnp.where(
+        position == sections - 1, embedded, mirrored(outbox[0], "section", sections - 2)
+    )
+    fetched = mirrored(stash_held[0], "section", sections - 1)
     x_full, gain_full = (
         lax.all_gather(x_shard, "tensor", axis=1, tiled=True),
         lax.all_gather(norm_gain, "tensor", axis=1, tiled=True),
@@ -102,12 +83,10 @@
         partial_value.astype(jnp.bfloat16), "tensor", scatter_dimension=1, tiled=True
     ).astype(jnp.float32)
     section_out = (x_shard.astype(jnp.float32) + mixed).astype(jnp.bfloat16)
-    fetched = fetch_shard_back(stash_held[0], bits)
     stash_full, grad_full = (
         lax.all_gather(fetched, "tensor", axis=1, tiled=True),
         lax.all_gather(grad_shard, "tensor", axis=1, tiled=True),
     )
-    stash_shard = lax.dynamic_slice_in_dim(stash_full, column * width, width, 1)
     inv_back, query_back, keyval_back = normalize_project(stash_full, gain_full, wq, wkv)
     prob, prob_low, split, keys, values, unused = attend_local(query_back, keyval_back, heads)
     seq = stash_full.shape[0]
@@ -133,12 +112,17 @@
     back_terms = back_terms + lax.dot_general(
         d_pairs, wkv, (((1,), (1,)), ((), ())), preferred_element_type=jnp.float32
     )
-    summed = lax.psum(back_terms.astype(jnp.bfloat16), "tensor").astype(jnp.float32)
-    scaled_full = summed * gain_full.astype(jnp.float32)
-    total = jnp.sum(scaled_full * stash_full.astype(jnp.float32), axis=-1, keepdims=True)
-    scaled = lax.dynamic_slice_in_dim(scaled_full, column * width, width, 1)
+    gain_float = gain_full.astype(jnp.float32)
+    own_total = jnp.sum(
+        back_terms * gain_float * stash_full.astype(jnp.float32), axis=-1, keepdims=True
+    )
+    total = lax.psum(own_total, "tensor")
+    summed = lax.psum_scatter(
+        back_terms.astype(jnp.bfloat16), "tensor", scatter_dimension=1, tiled=True
+    ).astype(jnp.float32)
+    scaled = summed * norm_gain.astype(jnp.float32)
     correction = total / D
-    stash_float = stash_shard.astype(jnp.float32)
+    stash_float = fetched.astype(jnp.float32)
     result = (
         grad_shard.astype(jnp.float32) + inv_back * scaled - stash_float * inv_back**3 * correction
     )

time: 301 us -> 241 us (0.80)
  waiting for transfers between devices: 168 us -> 114 us
  starting transfers between devices: 25.1 us -> 12.6 us
  blocking collectives: 37.7 us -> 47.9 us
    reduce_scatter x0 -> x1, waiting for transfers between devices: none -> 43.4 us  [local(): lax.psum_scatter(back_terms.astype(jnp.bfloat16), 'tensor', scatter_dimen...]
    ppermute x10 -> x2, waiting for transfers between devices: 54.1 us -> 13.5 us  [mirrored(): lax.ppermute(value, axis, [(source, last - source) for source in range(la...]
    reduce_scatter x1, waiting for transfers between devices: 39 us -> 4.15 us  [local(): lax.psum_scatter(partial_value.astype(jnp.bfloat16), 'tensor', scatter_di...]
    psum x1 -> x0, waiting for transfers between devices: 31 us -> none  [local(): lax.psum(back_terms.astype(jnp.bfloat16), 'tensor').astype(jnp.float32)]
    all_gather x1, waiting for transfers between devices: 0.01 us -> 30.3 us  [local(): lax.all_gather(grad_shard, 'tensor', axis=1, tiled=True)]
    all_gather x1, waiting for transfers between devices: 30.6 us -> 11.7 us  [local(): lax.all_gather(fetched, 'tensor', axis=1, tiled=True)]
    psum x0 -> x1, blocking collectives: none -> 15.3 us  [local(): total = lax.psum(own_total, 'tensor')]
    ppermute x10 -> x2, starting transfers between devices: 19.7 us -> 8.33 us  [mirrored(): lax.ppermute(value, axis, [(source, last - source) for source in range(la...]
  transfers between devices with their start and end apart: 17 -> 9, of which waited for: 15 -> 8; matrix products, arithmetic and copies ran while one was open for 8% -> 19% of each run, Pallas kernels for 0% -> 0%
where the time goes in v1:
time: 241 us; the launch traced here: 237 us
  waiting for transfers between devices  114 us (47%)
  blocking collectives  47.9 us (20%)
  matrix products  36.6 us (15%)
  between operations  14.1 us (6%)
  starting transfers between devices  12.6 us (5%)
  other arithmetic  11.1 us (5%)
    reduce_scatter x1, waiting for transfers between devices, local(): lax.psum_scatter(back_terms.astype(jnp.bfloat16), 'tensor', scatter_dimen...  43.4 us
    all_gather x1, blocking collectives, local(): lax.all_gather(norm_gain, 'tensor', axis=1, tiled=True)  32.6 us
    all_gather x1, waiting for transfers between devices, local(): lax.all_gather(grad_shard, 'tensor', axis=1, tiled=True)  30.3 us
    psum x1, blocking collectives, local(): total = lax.psum(own_total, 'tensor')  15.3 us
    ppermute x2, waiting for transfers between devices, mirrored(): lax.ppermute(value, axis, [(source, last - source) for source in range(la...  13.5 us
    all_gather x1, waiting for transfers between devices, local(): lax.all_gather(fetched, 'tensor', axis=1, tiled=True)  11.7 us
    ppermute x2, waiting for transfers between devices, shifted(): lax.ppermute(value, axis, [(source, source + steps) for source in range(f...  10.7 us
    ppermute x2, starting transfers between devices, mirrored(): lax.ppermute(value, axis, [(source, last - source) for source in range(la...  8.33 us
  transfers between devices with their start and end apart: 9, of which 8 were waited for; matrix products, arithmetic and copies ran while one was open for 19% of the time, Pallas kernels for 0%

profile of v1, /device:TPU:33, one launch (start us, length us, event | category | flops | bytes accessed | tf_op | source)
XLA Modules:
  0.0 237.1 jit_solution(12814726346854970629)
XLA Ops:
  7.2 0.0 copy-start
  7.2 0.0 all-gather.4.cloned.1.call-start
  7.2 7.2 %collective-permute-start.1 = (bf16[256,512]{1,0:T(8,128)(2,1)}, bf16[256,512]{1,0:T(8,128)(2,1)S(1)}, u32[]{:S(2)}, u32[]{:S(2)}) collective-permute-start(bf16[256,512]{1,0:T(8,128)(2,1)} %bitcast.163), channel_id=1, source_target_pairs={{0,240},{8,232},{16,224},{24,216},{32,208},{40,200},{48,192},{56,1... | collective-permute-start | bytes 786440 | tf_op jit(solution)/shard_map/ppermute | solution.py:14
  14.5 1.9 collective-permute-start
  16.4 4.1 %collective-permute-done.1 = bf16[256,512]{1,0:T(8,128)(2,1)S(1)} collective-permute-done((bf16[256,512]{1,0:T(8,128)(2,1)}, bf16[256,512]{1,0:T(8,128)(2,1)S(1)}, u32[]{:S(2)}, u32[]{:S(2)}) %collective-permute-start.1) | collective-permute-done | bytes 262176 | tf_op jit(solution)/shard_map/ppermute | solution.py:14
  20.5 2.9 %collective-permute-done = bf16[256,512]{1,0:T(8,128)(2,1)S(1)} collective-permute-done((bf16[256,512]{1,0:T(8,128)(2,1)}, bf16[256,512]{1,0:T(8,128)(2,1)S(1)}, u32[]{:S(2)}, u32[]{:S(2)}) %collective-permute-start) | collective-permute-done | bytes 262176 | tf_op jit(solution)/shard_map/ppermute | solution.py:20
  23.4 1.8 select_bitcast_fusion
  25.2 0.0 all-gather.4.cloned.1.call-update
  25.2 0.0 all-gather.6.cloned.1.call-start
  25.3 1.1 collective-permute-start.3
  26.4 9.4 %collective-permute-done.3 = bf16[256,512]{1,0:T(8,128)(2,1)S(1)} collective-permute-done((bf16[256,512]{1,0:T(8,128)(2,1)}, bf16[256,512]{1,0:T(8,128)(2,1)S(1)}, u32[]{:S(2)}, u32[]{:S(2)}) %collective-permute-start.3) | collective-permute-done | bytes 262176 | tf_op jit(solution)/shard_map/ppermute | solution.py:14
  35.7 0.7 copy-done.8
  36.4 0.0 all-gather.6.cloned.1.call-update
  36.5 0.0 all-gather.8.cloned.1.call-start
  36.5 1.9 collective-permute-start.2
  38.4 7.8 %collective-permute-done.2 = bf16[256,512]{1,0:T(8,128)(2,1)S(1)} collective-permute-done((bf16[256,512]{1,0:T(8,128)(2,1)}, bf16[256,512]{1,0:T(8,128)(2,1)S(1)}, u32[]{:S(2)}, u32[]{:S(2)}) %collective-permute-start.2) | collective-permute-done | bytes 262176 | tf_op jit(solution)/shard_map/ppermute | solution.py:20
  46.3 0.7 broadcast_select_fusion
  47.0 0.0 all-gather.8.cloned.1.call-update
  47.1 0.0 reduce-scatter.3.cloned.1.call-start
  47.1 32.6 %all_gather.13 = bf16[1,4096]{1,0:T(2,128)(2,1)S(1)} all-gather(bf16[1,512]{1,0:T(2,128)(2,1)} %param.14), channel_id=1, replica_groups=mesh['section'=32,'tensor'=8] {'tensor'}, dimensions={1}, use_global_device_ids=true | all-gather | bytes 9216 | tf_op jit(solution)/shard_map/all_gather | solution.py:77
  79.8 0.0 all-gather.4.cloned.1.call-done
  79.8 0.0 copy-start.3
  79.9 2.2 fusion.3
  82.1 0.0 copy-done
  82.1 2.9 %fusion.54 = bf16[256,256]{1,0:T(8,128)(2,1)S(1)} fusion(bf16[1,4096,256]{2,1,0:T(8,128)(2,1)S(1)} %copy-done, bf16[256,4096]{1,0:T(8,128)(2,1)} %all-gather.4.cloned.1.call-done, f32[4096]{0:T(1024)S(1)} %bitcast.155, f32[256]{0:T(256)S(1)} %add_rsqrt_fusion.1), kind=kOutput, calls=%fused_computation.54 | convolution fusion | flops 541130752 | bytes 4342784 | tf_op jit(solution)/shard_map/dot_general | solution.py:28
  85.1 0.0 copy-done.3
  85.1 0.0 copy-done.7
  85.1 0.0 copy-start.11
  85.1 1.3 fusion.51
  86.4 0.5 fusion.109
  86.9 1.1 fusion.34
  88.0 1.2 convolution_convert_fusion.2
  89.3 4.8 %convolution_convert_fusion = bf16[256,4096]{1,0:T(8,128)(2,1)} fusion(bf16[256,512]{0,1:T(8,128)(2,1)S(1)} %bitcast.154, bf16[1,512,4096]{2,1,0:T(8,128)(2,1)} %param.17), kind=kOutput, calls=%fused_computation.9 | convolution fusion | flops 1074790400 | bytes 6553600 | tf_op jit(solution)/shard_map/dot_general | solution.py:81
  94.1 0.0 reduce-scatter.3.cloned.1.call-update
  94.1 0.2 reduce-scatter.5.cloned.1.call-start
  94.3 11.7 %all-gather.6.cloned.1.call-done = bf16[256,4096]{1,0:T(8,128)(2,1)} async-done(((bf16[256,512]{1,0:T(8,128)(2,1)}), bf16[256,4096]{1,0:T(8,128)(2,1)}) %all-gather.6.cloned.1.call-update) | async-done | bytes 2097168 | tf_op jit(solution)/shard_map/all_gather | solution.py:87
  106.1 2.1 fusion.6
  108.1 0.6 multiply_multiply_fusion
  108.7 3.0 %fusion.57 = bf16[256,256]{1,0:T(8,128)(2,1)} fusion(bf16[1,4096,256]{2,1,0:T(8,128)(2,1)S(1)} %copy-done, bf16[256,4096]{1,0:T(8,128)(2,1)} %all-gather.6.cloned.1.call-done, f32[256]{0:T(256)S(1)} %get-tuple-element.8, f32[4096]{0:T(1024)S(1)} %bitcast.157), kind=kOutput, calls=%fused_computation.55 | convolution fusion | flops 541130752 | bytes 4342784 | tf_op jit(solution)/shard_map/dot_general | solution.py:28
  111.7 30.3 %all-gather.8.cloned.1.call-done = bf16[256,4096]{1,0:T(8,128)(2,1)} async-done(((bf16[256,512]{1,0:T(8,128)(2,1)}), bf16[256,4096]{1,0:T(8,128)(2,1)}) %all-gather.8.cloned.1.call-update) | async-done | bytes 2097168 | tf_op jit(solution)/shard_map/all_gather | solution.py:88
  142.0 4.3 %fusion.45 = bf16[32,4,8,128]{3,2,1,0:T(8,128)(2,1)S(1)} fusion(bf16[256,4096]{1,0:T(8,128)(2,1)} %all-gather.8.cloned.1.call-done, bf16[1,512,4096]{2,1,0:T(8,128)(2,1)} %param.17), kind=kOutput, calls=%fused_computation.51 | convolution fusion | flops 1073872896 | bytes 6553600 | tf_op jit(solution)/shard_map/dot_general | solution.py:93
  146.3 0.0 copy-done.12
  146.3 0.0 copy-start.10
  146.3 0.3 convolution_bitcast_fusion
  146.6 0.0 copy-done.15
  146.6 0.0 copy-done.1
  146.6 0.1 copy-done.4
  146.8 2.0 fusion.48
  148.8 0.0 copy-done.10
  148.8 3.0 %fusion.112 = (f32[4,256]{1,0:T(4,128)}, f32[4,256,256]{1,2,0:T(8,128)}) fusion(pred[256,256]{0,1:T(8,128)(4,1)S(1)} %iota_compare_fusion, bf16[32,4,8,128]{3,2,1,0:T(8,128)(2,1)} %fusion.48, bf16[256,256]{1,0:T(8,128)(2,1)} %fusion.57), kind=kOutput, calls=%fused_computation.109 | convolution fusion | flops 68157696 | bytes 1445888 | tf_op jit(solution)/shard_map/sub | solution.py:44
  151.8 2.1 fusion.60
  153.9 2.1 convolution_convert_fusion.1
  155.9 1.8 fusion.61
  157.7 3.7 %fusion.13 = f32[256,4096]{1,0:T(8,128)S(1)} fusion(bf16[256,512]{0,1:T(8,128)(2,1)S(1)} %bitcast.153, bf16[1,4096,512]{2,1,0:T(8,128)(2,1)} %param.15), kind=kOutput, calls=%fused_computation.20 | convolution fusion | flops 1073741824 | bytes 8650752 | tf_op jit(solution)/shard_map/dot_general | solution.py:109
  161.5 0.0 copy-done.2
  161.5 0.0 copy-start.13
  161.5 0.0 copy-start.5
  161.5 2.5 %fusion.9 = (f32[256]{0:T(256)S(1)}, bf16[256,4096]{1,0:T(8,128)(2,1)}) fusion(bf16[256,4096]{1,0:T(8,128)(2,1)S(1)} %copy-done.2, f32[4096]{0:T(1024)S(1)} %bitcast.159, f32[256,4096]{1,0:T(8,128)S(1)} %fusion.13, bf16[1,4096,256]{2,1,0:T(8,128)(2,1)S(1)} %copy-done, bf16[256,128]{1,0:T(8,128)(2,1)S(1)} %fusion.61, bf16[256,128]{1,0:T(8,128)(2,1)S(1)} %fusion.60), kind=kOutput, calls=%fused_computation.16 | convolution fusion | flops 543424256 | bytes 10634240 | tf_op jit(solution)/shard_map/dot_general | solution.py:112
  164.1 0.0 reduce-scatter.5.cloned.1.call-update
  164.1 15.3 %psum.7 = f32[256,1]{0,1:T(1,128)S(1)} all-reduce(f32[256,1]{0,1:T(1,128)S(1)} %bitcast.162), channel_id=1, replica_groups=mesh['section'=32,'tensor'=8] {'tensor'}, use_global_device_ids=true, to_apply=%region_10.11 | all-reduce | flops 256 | bytes 2048 | tf_op jit(solution)/shard_map/psum | solution.py:119
  179.4 4.1 %reduce-scatter.3.cloned.1.call-done = bf16[256,512]{1,0:T(8,128)(2,1)} async-done(((bf16[256,4096]{1,0:T(8,128)(2,1)}), bf16[256,512]{1,0:T(8,128)(2,1)}) %reduce-scatter.3.cloned.1.call-update) | async-done | bytes 262160 | tf_op jit(solution)/shard_map/reduce_scatter | solution.py:82
  183.5 1.7 fusion.73
  185.3 43.4 %reduce-scatter.5.cloned.1.call-done = bf16[256,512]{1,0:T(8,128)(2,1)} async-done(((bf16[256,4096]{1,0:T(8,128)(2,1)}), bf16[256,512]{1,0:T(8,128)(2,1)}) %reduce-scatter.5.cloned.1.call-update) | async-done | bytes 262160 | tf_op jit(solution)/shard_map/reduce_scatter | solution.py:120
  228.7 1.9 fusion.74
  (23 shorter events, 0.1 us)
Async XLA Ops:
  7.2 74.9 %copy-start = (bf16[1,4096,256]{2,1,0:T(8,128)(2,1)S(1)}, bf16[1,4096,256]{2,1,0:T(8,128)(2,1)}, u32[]{:S(2)}) copy-start(bf16[1,4096,256]{2,1,0:T(8,128)(2,1)} %param.16) | copy-start | bytes 6291460
  7.2 72.7 %all-gather.4.cloned.1.call-start = ((), (), s32[]{:S(2)}) async-start(), calls=%async_computation.2 | async-start | bytes 2359296 | tf_op jit(solution)/shard_map/all_gather | solution.py:76
  7.2 13.3 %collective-permute-start.1 = (bf16[256,512]{1,0:T(8,128)(2,1)}, bf16[256,512]{1,0:T(8,128)(2,1)S(1)}, u32[]{:S(2)}, u32[]{:S(2)}) collective-permute-start(bf16[256,512]{1,0:T(8,128)(2,1)} %bitcast.163), channel_id=1, source_target_pairs={{0,240},{8,232},{16,224},{24,216},{32,208},{40,200},{48,192},{56,1... | collective-permute-start | bytes 786440 | tf_op jit(solution)/shard_map/ppermute | solution.py:14
  14.5 9.0 %collective-permute-start = (bf16[256,512]{1,0:T(8,128)(2,1)}, bf16[256,512]{1,0:T(8,128)(2,1)S(1)}, u32[]{:S(2)}, u32[]{:S(2)}) collective-permute-start(bf16[256,512]{1,0:T(8,128)(2,1)} %bitcast.164), channel_id=1, source_target_pairs={{0,8},{8,16},{16,24},{24,32},{32,40},{40,48},{48,56},{56,64},{64,7... | collective-permute-start | bytes 786440 | tf_op jit(solution)/shard_map/ppermute | solution.py:20
  25.2 80.8 %all-gather.6.cloned.1.call-start = ((), (), s32[]{:S(2)}) async-start(), calls=%async_computation.4 | async-start | bytes 2359296 | tf_op jit(solution)/shard_map/all_gather | solution.py:87
  25.3 10.4 %collective-permute-start.3 = (bf16[256,512]{1,0:T(8,128)(2,1)}, bf16[256,512]{1,0:T(8,128)(2,1)S(1)}, u32[]{:S(2)}, u32[]{:S(2)}) collective-permute-start(bf16[256,512]{1,0:T(8,128)(2,1)} %bitcast.165), channel_id=1, source_target_pairs={{0,248},{8,240},{16,232},{24,224},{32,216},{40,208},{48,200},{56,1... | collective-permute-start | bytes 786440 | tf_op jit(solution)/shard_map/ppermute | solution.py:14
  35.7 0.7 copy-start.8
  36.5 105.6 %all-gather.8.cloned.1.call-start = ((), (), s32[]{:S(2)}) async-start(), calls=%async_computation.5 | async-start | bytes 2359296 | tf_op jit(solution)/shard_map/all_gather | solution.py:88
  36.5 9.8 %collective-permute-start.2 = (bf16[256,512]{1,0:T(8,128)(2,1)}, bf16[256,512]{1,0:T(8,128)(2,1)S(1)}, u32[]{:S(2)}, u32[]{:S(2)}) collective-permute-start(bf16[256,512]{1,0:T(8,128)(2,1)} %bitcast.166), channel_id=1, source_target_pairs={{8,0},{16,8},{24,16},{32,24},{40,32},{48,40},{56,48},{64,56},{72,6... | collective-permute-start | bytes 786440 | tf_op jit(solution)/shard_map/ppermute | solution.py:20
  47.1 136.5 %reduce-scatter.3.cloned.1.call-start = ((), (), s32[]{:S(2)}) async-start(), calls=%async_computation.3 | async-start | bytes 2359296 | tf_op jit(solution)/shard_map/reduce_scatter | solution.py:82
  79.8 5.2 %copy-start.3 = (bf16[1,4096,512]{2,1,0:T(8,128)(2,1)S(1)}, bf16[1,4096,512]{2,1,0:T(8,128)(2,1)}, u32[]{:S(2)}) copy-start(bf16[1,4096,512]{2,1,0:T(8,128)(2,1)} %param.15) | copy-start | bytes 12582916
  79.9 5.2 %copy-start.7 = (bf16[256,4096]{1,0:T(8,128)(2,1)S(1)}, bf16[256,4096]{1,0:T(8,128)(2,1)}, u32[]{:S(2)}) copy-start(bf16[256,4096]{1,0:T(8,128)(2,1)} %all-gather.4.cloned.1.call-done) | copy-start | bytes 6291460
  85.1 1.3 copy-start.11
  94.1 134.6 %reduce-scatter.5.cloned.1.call-start = ((), (), s32[]{:S(2)}) async-start(), calls=%async_computation.6 | async-start | bytes 2359296 | tf_op jit(solution)/shard_map/reduce_scatter | solution.py:120
  108.7 37.9 %copy-start.15 = (f32[256]{0:T(256)}, f32[256]{0:T(256)S(1)}, u32[]{:S(2)}) copy-start(f32[256]{0:T(256)S(1)} %get-tuple-element.8) | copy-start | bytes 3076
  142.0 4.3 %copy-start.12 = (bf16[256,256]{1,0:T(8,128)(2,1)S(1)}, bf16[256,256]{1,0:T(8,128)(2,1)}, u32[]{:S(2)}) copy-start(bf16[256,256]{1,0:T(8,128)(2,1)} %fusion.57) | copy-start | bytes 393220
  142.0 4.6 %copy-start.1 = (bf16[256,4096]{1,0:T(8,128)(2,1)S(1)}, bf16[256,4096]{1,0:T(8,128)(2,1)}, u32[]{:S(2)}) copy-start(bf16[256,4096]{1,0:T(8,128)(2,1)} %all-gather.6.cloned.1.call-done) | copy-start | bytes 6291460
  142.0 4.7 %copy-start.4 = (bf16[1,4096,512]{2,1,0:T(8,128)(2,1)S(1)}, bf16[1,4096,512]{2,1,0:T(8,128)(2,1)}, u32[]{:S(2)}) copy-start(bf16[1,4096,512]{2,1,0:T(8,128)(2,1)} %param.15) | copy-start | bytes 12582916
  146.3 2.5 %copy-start.10 = (bf16[32,4,8,128]{3,2,1,0:T(8,128)(2,1)}, bf16[32,4,8,128]{3,2,1,0:T(8,128)(2,1)S(1)}, u32[]{:S(2)}) copy-start(bf16[32,4,8,128]{3,2,1,0:T(8,128)(2,1)S(1)} %fusion.45) | copy-start | bytes 786436
  157.7 3.7 %copy-start.2 = (bf16[256,4096]{1,0:T(8,128)(2,1)S(1)}, bf16[256,4096]{1,0:T(8,128)(2,1)}, u32[]{:S(2)}) copy-start(bf16[256,4096]{1,0:T(8,128)(2,1)} %all-gather.6.cloned.1.call-done) | copy-start | bytes 6291460
  161.5 2.6 %copy-start.13 = (bf16[1,512]{1,0:T(2,128)(2,1)S(1)}, bf16[1,512]{1,0:T(2,128)(2,1)}, u32[]{:S(2)}) copy-start(bf16[1,512]{1,0:T(2,128)(2,1)} %param.14) | copy-start | bytes 3076
  161.5 22.1 %copy-start.5 = (bf16[256,512]{1,0:T(8,128)(2,1)S(1)}, bf16[256,512]{1,0:T(8,128)(2,1)}, u32[]{:S(2)}) copy-start(bf16[256,512]{1,0:T(8,128)(2,1)} %get-tuple-element.6) | copy-start | bytes 786436
  161.5 67.2 %copy-start.6 = (bf16[256,512]{1,0:T(8,128)(2,1)S(1)}, bf16[256,512]{1,0:T(8,128)(2,1)}, u32[]{:S(2)}) copy-start(bf16[256,512]{1,0:T(8,128)(2,1)} %broadcast_select_fusion) | copy-start | bytes 786436
  161.5 67.2 %copy-start.9 = (bf16[256,512]{1,0:T(8,128)(2,1)S(1)}, bf16[256,512]{1,0:T(8,128)(2,1)}, u32[]{:S(2)}) copy-start(bf16[256,512]{1,0:T(8,128)(2,1)} %copy-done.8) | copy-start | bytes 786436
  161.5 67.2 %copy-start.14 = (f32[256]{0:T(256)S(1)}, f32[256]{0:T(256)}, u32[]{:S(2)}) copy-start(f32[256]{0:T(256)} %get-tuple-element.7) | copy-start | bytes 3076
  161.5 67.2 %copy-start.16 = (f32[256]{0:T(256)S(1)}, f32[256]{0:T(256)}, u32[]{:S(2)}) copy-start(f32[256]{0:T(256)} %copy-done.15) | copy-start | bytes 3076
Sparse Core Ops, SparseCore 0:
  25.4 44.5 all-gather.3
  71.8 34.2 all-gather.5
  107.9 34.0 all-gather.7
  144.4 39.0 reduce-scatter.2
  185.9 42.7 reduce-scatter.4

commit v2 on v1

v2 whole, which is shorter than its diff:
```python
import jax
import jax.numpy as jnp
from jax import lax
from jax.experimental import pallas as pl
from jax.experimental.pallas import tpu as pltpu
from jax.sharding import PartitionSpec as P

HEAD = 128
EPS = 1e-05
F32 = jnp.float32
BF16 = jnp.bfloat16
NT = (((1,), (1,)), ((), ()))
TN = (((0,), (0,)), ((), ()))
STASH, GRAD, FRESH = 0, 1, 2


def dot(a, b, dims=(((1,), (0,)), ((), ()))):
    return lax.dot_general(a, b, dims, preferred_element_type=F32)


def kernel(
    embedded,
    outbox,
    loss_grad,
    grad_outbox,
    stash,
    gain,
    w_query,
    w_keyval,
    w_out,
    section_out,
    evicted,
    input_grad,
    full,
    gain_raw,
    gains,
    wq,
    wkv,
    wo,
    acc_q,
    acc_kv,
    acc_g,
    inv_ref,
    query,
    keyval,
    dquery_h,
    flat,
    dpair,
    dpair_low,
    row_sums,
    sib_out,
    sib_in,
    sums,
    own,
    ring_in,
    last_in,
    result,
    weight_sem,
    local_sem,
    gain_send,
    gain_recv,
    row_send,
    row_recv,
    near_send,
    near_recv,
    far_send,
    far_recv,
    sib_send,
    sib_recv,
    evict_send,
    evict_recv,
    rs_sib_send,
    rs_sib_recv,
    rs_send,
    rs_recv,
):
    sections = lax.axis_size("section")
    tensors = lax.axis_size("tensor")
    chips = tensors // 2
    s = lax.axis_index("section")
    t = lax.axis_index("tensor")
    seq, width = outbox.shape[1], outbox.shape[2]
    half = seq // 2
    features = width * tensors
    heads = width // HEAD
    halves = [pl.ds(0, half), pl.ds(half, half)]
    parity = lax.rem(s, 2)
    chip = t // 2
    core = lax.rem(t, 2)

    def member(chip_index, core_index):
        return 2 * lax.rem(chip_index, chips) + core_index

    above = member(chip + parity, core)
    below = member(chip + parity + chips - 1, core)
    up = member(chip + 1, core)
    down = member(chip + chips - 1, core)
    sibling = member(chip, 1 - core)
    targets = [
        sections - 1 - s,
        lax.rem(s + sections - 1, sections),
        lax.rem(s + 1, sections),
    ]
    mirror = sections - 2 - s
    goes_away = (s != sections - 1) & (mirror != s)
    stays = mirror == s
    final = s == sections - 1

    pending = []

    def remote(src, dst, send, recv, section, tensor):
        return pltpu.make_async_remote_copy(
            src_ref=src,
            dst_ref=dst,
            send_sem=send,
            recv_sem=recv,
            device_id=(section, tensor),
            device_id_type=pl.DeviceIdType.MESH,
        )

    def launch(*args):
        copy = remote(*args)
        copy.start()
        pending.append(copy)

    def arrived(ref, send, recv):
        remote(ref, ref, send, recv, s, sibling).wait_recv()

    barrier = pltpu.get_barrier_semaphore()
    peers = [(s, lax.rem(t + step, tensors)) for step in range(1, tensors)]
    peers += [(section, tensor) for section in targets for tensor in (above, below)]
    for peer in peers:
        pl.semaphore_signal(
            barrier, inc=1, device_id=peer, device_id_type=pl.DeviceIdType.MESH
        )

    @pl.when(goes_away)
    def _():
        pl.semaphore_signal(
            barrier, inc=1, device_id=(mirror, t), device_id_type=pl.DeviceIdType.MESH
        )

    gain_copy = pltpu.make_async_copy(gain, gain_raw, local_sem.at[0])
    gain_copy.start()
    weights = [
        pltpu.make_async_copy(w_query, wq, weight_sem.at[0]),
        pltpu.make_async_copy(w_keyval, wkv, weight_sem.at[1]),
    ]
    for block in range(tensors):
        weights.append(
            pltpu.make_async_copy(
                w_out.at[:, pl.ds(block * width, width)], wo.at[block], weight_sem.at[2 + block]
            )
        )
    for copy in weights:
        copy.start()
    gain_copy.wait()
    gains[t] = gain_raw[...].astype(F32)

    @pl.when(goes_away)
    def _():
        pl.semaphore_wait(barrier, len(peers) + 1)

    @pl.when(jnp.logical_not(goes_away))
    def _():
        pl.semaphore_wait(barrier, len(peers))

    def near(which, src):
        copies = []
        for part, rows in enumerate(halves):
            for side, tensor in enumerate((above, below)):
                copies.append(
                    remote(
                        src.at[rows],
                        full.at[which, t, rows],
                        near_send.at[which, side, part],
                        near_recv.at[which, side, part],
                        targets[which],
                        tensor,
                    )
                )
        return copies

    def near_start(which, usual, other, use_other):
        if other is None:
            for copy in near(which, usual):
                copy.start()
        else:

            @pl.when(use_other)
            def _():
                for copy in near(which, other):
                    copy.start()

            @pl.when(jnp.logical_not(use_other))
            def _():
                for copy in near(which, usual):
                    copy.start()

        pending.extend(near(which, usual))

    low = lax.rem(chip + parity + chips - 1, chips)
    high = lax.rem(chip + parity, chips)
    slots = [low, high, lax.rem(low + chips - 1, chips), lax.rem(high + 1, chips)]

    def pass_near(which):
        for part, rows in enumerate(halves):
            for side, ahead in enumerate((up, down)):
                here = full.at[which, 2 * slots[side] + core, rows]
                arrived(here, near_send.at[which, side, part], near_recv.at[which, side, part])
                launch(
                    here,
                    here,
                    far_send.at[which, side, part],
                    far_recv.at[which, side, part],
                    s,
                    ahead,
                )
                launch(
                    here,
                    here,
                    sib_send.at[which, side, part],
                    sib_recv.at[which, side, part],
                    s,
                    sibling,
                )

    def pass_far(which):
        for part, rows in enumerate(halves):
            for side in range(2):
                here = full.at[which, 2 * slots[2 + side] + core, rows]
                arrived(here, far_send.at[which, side, part], far_recv.at[which, side, part])
                launch(
                    here,
                    here,
                    sib_send.at[which, 2 + side, part],
                    sib_recv.at[which, 2 + side, part],
                    s,
                    sibling,
                )

    def gathered(which):
        for part, rows in enumerate(halves):
            for place in range(4):
                here = full.at[which, 2 * slots[place] + 1 - core, rows]
                arrived(here, sib_send.at[which, place, part], sib_recv.at[which, place, part])

    def project(which):
        def squares(block, total):
            value = full[which, block].astype(F32)
            value = value * value
            for piece in range(width // 128):
                total = total + value[:, piece * 128 : (piece + 1) * 128]
            return total

        total = lax.fori_loop(0, tensors, squares, jnp.zeros((seq, 128), F32))
        inv = lax.rsqrt(jnp.sum(total, axis=-1, keepdims=True) / features + EPS)
        acc_q[...] = jnp.zeros_like(acc_q)
        acc_kv[...] = jnp.zeros_like(acc_kv)

        def step(block, carry):
            normed = (full[which, block].astype(F32) * inv * gains[block]).astype(BF16)
            acc_q[...] += dot(normed, wq[block])
            acc_kv[...] += dot(normed, wkv[block])
            return carry

        lax.fori_loop(0, tensors, step, 0)
        for head in range(heads):
            query[head] = acc_q[:, head * HEAD : (head + 1) * HEAD].astype(BF16)
        for side in range(2):
            keyval[side] = acc_kv[:, side * HEAD : (side + 1) * HEAD].astype(BF16)
        return inv

    def probability(head):
        scores = dot(query[head], keyval[0], NT) * HEAD ** (-0.5)
        rows = lax.broadcasted_iota(jnp.int32, (seq, seq), 0)
        cols = lax.broadcasted_iota(jnp.int32, (seq, seq), 1)
        scores = jnp.where(rows >= cols, scores, -1e30)
        top = jnp.max(scores, axis=-1, keepdims=True)
        raised = jnp.exp(scores - top)
        return raised / jnp.sum(raised, axis=-1, keepdims=True)

    def chip_at(turn):
        return lax.rem(chip + 2 + chips - turn, chips)

    def reduce_start(which, term):
        def for_sibling(turn, carry):
            sib_out[which, turn] = term(2 * chip_at(turn) + 1 - core).astype(BF16)
            remote(
                sib_out.at[which, turn],
                sib_in.at[which, turn],
                rs_sib_send.at[which, turn],
                rs_sib_recv.at[which, turn],
                s,
                sibling,
            ).start()
            return carry

        lax.fori_loop(0, chips, for_sibling, 0)
        for turn in range(chips):
            pending.append(
                remote(
                    sib_out.at[which, turn],
                    sib_in.at[which, turn],
                    rs_sib_send.at[which, turn],
                    rs_sib_recv.at[which, turn],
                    s,
                    sibling,
                )
            )
        opening = [
            (0, 0, 0, ring_in.at[which, 0], up),
            (0, 1, 1, ring_in.at[which, 1], down),
            (1, 1, 2, last_in.at[which, 0, halves[1]], up),
            (3, 0, 3, last_in.at[which, 1, halves[0]], down),
        ]

        def sends(turn):
            return [
                remote(
                    sums.at[which, at, halves[part]],
                    dst,
                    rs_send.at[which, sem],
                    rs_recv.at[which, sem],
                    s,
                    tensor,
                )
                for at, part, sem, dst, tensor in opening
                if at == turn
            ]

        def for_self(turn, carry):
            mine = term(2 * chip_at(turn) + core)
            arrived(
                sib_in.at[which, turn], rs_sib_send.at[which, turn], rs_sib_recv.at[which, turn]
            )
            total = mine + sib_in[which, turn].astype(F32)
            sums[which, turn] = total.astype(BF16)

            @pl.when(turn == 2)
            def _():
                own[which] = total

            for at in (0, 1, 3):

                @pl.when(turn == at)
                def _():
                    for copy in sends(at):
                        copy.start()

            return carry

        lax.fori_loop(0, chips, for_self, 0)
        for at in (0, 1, 3):
            pending.extend(sends(at))

    def reduce_middle(which):
        for side, (turn, part, ahead) in enumerate(((1, 0, up), (3, 1, down))):
            rows = halves[part]
            arrived(ring_in.at[which, side], rs_send.at[which, side], rs_recv.at[which, side])
            sums[which, turn, rows] = (
                sums[which, turn, rows].astype(F32) + ring_in[which, side].astype(F32)
            ).astype(BF16)
            launch(
                sums.at[which, turn, rows],
                last_in.at[which, side, rows],
                rs_send.at[which, 4 + side],
                rs_recv.at[which, 4 + side],
                s,
                ahead,
            )

    def reduce_end(which):
        arrived(last_in.at[which, 0, halves[1]], rs_send.at[which, 2], rs_recv.at[which, 2])
        arrived(last_in.at[which, 1, halves[0]], rs_send.at[which, 3], rs_recv.at[which, 3])
        arrived(last_in.at[which, 0, halves[0]], rs_send.at[which, 4], rs_recv.at[which, 4])
        arrived(last_in.at[which, 1, halves[1]], rs_send.at[which, 5], rs_recv.at[which, 5])
        return own[which] + last_in[which, 0].astype(F32) + last_in[which, 1].astype(F32)

    near_start(STASH, stash.at[0], None, None)
    for step in range(1, tensors):
        launch(
            gains.at[t],
            gains.at[t],
            gain_send.at[step],
            gain_recv.at[step],
            s,
            lax.rem(t + step, tensors),
        )
    near_start(GRAD, grad_outbox.at[0], loss_grad, s == 0)

    evict_copy = remote(outbox.at[0], evicted.at[0], evict_send, evict_recv, mirror, t)

    @pl.when(goes_away)
    def _():
        evict_copy.start()

    @pl.when(stays)
    def _():
        pltpu.make_async_copy(outbox.at[0], evicted.at[0], local_sem.at[1]).start()

    @pl.when(final)
    def _():
        pltpu.make_async_copy(embedded, evicted.at[0], local_sem.at[1]).start()

    pass_near(STASH)
    near_start(FRESH, outbox.at[0], embedded, final)
    pass_far(STASH)
    pass_near(GRAD)
    for step in range(1, tensors):
        here = gains.at[lax.rem(t + tensors - step, tensors)]
        arrived(here, gain_send.at[step], gain_recv.at[step])
    for copy in weights:
        copy.wait()
    gathered(STASH)
    inv_back = project(STASH)
    inv_ref[...] = jnp.broadcast_to(inv_back, inv_ref.shape)
    pass_far(GRAD)
    pass_near(FRESH)
    gathered(GRAD)

    acc_g[...] = jnp.zeros_like(acc_g)

    def pull_back(block, carry):
        acc_g[...] += dot(full[GRAD, block], wo[block], NT)
        return carry

    lax.fori_loop(0, tensors, pull_back, 0)
    for head in range(heads):
        dquery_h[head] = acc_g[:, head * HEAD : (head + 1) * HEAD].astype(BF16)
    dpair[...] = jnp.zeros_like(dpair)

    def head_back(head, total):
        prob = probability(head)
        d_head = dquery_h[head]
        d_prob = dot(d_head, keyval[1], NT)
        d_score = prob * (d_prob - jnp.sum(prob * d_prob, axis=-1, keepdims=True))
        d_score = (d_score * HEAD ** (-0.5)).astype(BF16)
        d_query = dot(d_score, keyval[0]).astype(BF16)
        dpair[0] += dot(d_score, query[head], TN)
        dpair[1] += dot(prob.astype(BF16), d_head, TN)
        dquery_h[head] = d_query
        return total + d_query.astype(F32) * query[head].astype(F32)

    total = lax.fori_loop(0, heads, head_back, jnp.zeros((seq, HEAD), F32))
    for head in range(heads):
        flat[:, head * HEAD : (head + 1) * HEAD] = dquery_h[head]
    for side in range(2):
        d_low = dpair[side].astype(BF16)
        dpair_low[:, side * HEAD : (side + 1) * HEAD] = d_low
        total = total + d_low.astype(F32) * keyval[side].astype(F32)
    row_sums[t] = jnp.sum(total.T, axis=0, keepdims=True)
    for step in range(1, tensors):
        launch(
            row_sums.at[t],
            row_sums.at[t],
            row_send.at[step],
            row_recv.at[step],
            s,
            lax.rem(t + step, tensors),
        )

    def back_term(block):
        return dot(flat[...], wq[block], NT) + dot(dpair_low[...], wkv[block], NT)

    reduce_start(0, back_term)
    pass_far(FRESH)
    gathered(FRESH)
    project(FRESH)
    reduce_middle(0)

    def head_forward(head, carry):
        dquery_h[head] = dot(probability(head).astype(BF16), keyval[1]).astype(BF16)
        return carry

    lax.fori_loop(0, heads, head_forward, 0)
    for head in range(heads):
        flat[:, head * HEAD : (head + 1) * HEAD] = dquery_h[head]

    def forward_term(block):
        return dot(flat[...], wo[block])

    reduce_start(1, forward_term)

    summed = reduce_end(0)
    for step in range(1, tensors):
        here = row_sums.at[lax.rem(t + tensors - step, tensors)]
        arrived(here, row_send.at[step], row_recv.at[step])
    row = row_sums[0]
    for block in range(1, tensors):
        row = row + row_sums[block]
    column = jnp.broadcast_to(row, (128, seq)).T[:, :1]
    inv = inv_ref[:, :1]
    result[0] = (
        full[GRAD, t].astype(F32)
        + inv * (summed * gains[t])
        - full[STASH, t].astype(F32) * (inv * inv * column / features)
    ).astype(BF16)
    grad_copy = pltpu.make_async_copy(result.at[0], input_grad.at[0], local_sem.at[2])
    grad_copy.start()
    reduce_middle(1)

    @pl.when(goes_away)
    def _():
        evict_copy.wait()

    @pl.when(jnp.logical_not(goes_away))
    def _():
        pltpu.make_async_copy(outbox.at[0], evicted.at[0], local_sem.at[1]).wait()

    grad_copy.wait()
    mixed = reduce_end(1)
    result[1] = (full[FRESH, t].astype(F32) + mixed).astype(BF16)
    out_copy = pltpu.make_async_copy(result.at[1], section_out.at[0], local_sem.at[3])
    out_copy.start()
    for copy in pending:
        copy.wait_send()
    out_copy.wait()


def local(
    embedded, outbox, loss_grad, grad_outbox, stash_held, norm_gain, w_query, w_keyval, w_out
):
    tensors = lax.axis_size("tensor")
    chips = tensors // 2
    _, seq, width = outbox.shape
    half = seq // 2
    heads = width // HEAD
    shard = jax.ShapeDtypeStruct(outbox.shape, BF16)
    dma = pltpu.SemaphoreType.DMA
    anywhere = pl.BlockSpec(memory_space=pl.ANY)
    return pl.pallas_call(
        kernel,
        out_shape=(shard, shard, shard),
        in_specs=[anywhere] * 9,
        out_specs=(anywhere, anywhere, anywhere),
        scratch_shapes=[
            pltpu.VMEM((3, tensors, seq, width), BF16),
            pltpu.VMEM((1, width), BF16),
            pltpu.VMEM((tensors, 1, width), F32),
            pltpu.VMEM((tensors, width, width), BF16),
            pltpu.VMEM((tensors, width, 2 * HEAD), BF16),
            pltpu.VMEM((tensors, width, width), BF16),
            pltpu.VMEM((seq, width), F32),
            pltpu.VMEM((seq, 2 * HEAD), F32),
            pltpu.VMEM((seq, width), F32),
            pltpu.VMEM((seq, 128), F32),
            pltpu.VMEM((heads, seq, HEAD), BF16),
            pltpu.VMEM((2, seq, HEAD), BF16),
            pltpu.VMEM((heads, seq, HEAD), BF16),
            pltpu.VMEM((seq, width), BF16),
            pltpu.VMEM((2, seq, HEAD), F32),
            pltpu.VMEM((seq, 2 * HEAD), BF16),
            pltpu.VMEM((tensors, 1, seq), F32),
            pltpu.VMEM((2, chips, seq, width), BF16),
            pltpu.VMEM((2, chips, seq, width), BF16),
            pltpu.VMEM((2, chips, seq, width), BF16),
            pltpu.VMEM((2, seq, width), F32),
            pltpu.VMEM((2, 2, half, width), BF16),
            pltpu.VMEM((2, 2, seq, width), BF16),
            pltpu.VMEM((2, seq, width), BF16),
            dma((2 + tensors,)),
            dma((4,)),
            dma((tensors,)),
            dma((tensors,)),
            dma((tensors,)),
            dma((tensors,)),
            dma((3, 2, 2)),
            dma((3, 2, 2)),
            dma((3, 2, 2)),
            dma((3, 2, 2)),
            dma((3, 4, 2)),
            dma((3, 4, 2)),
            dma,
            dma,
            dma((2, chips)),
            dma((2, chips)),
            dma((2, 6)),
            dma((2, 6)),
        ],
        compiler_params=pltpu.CompilerParams(
            collective_id=0, has_side_effects=True, vmem_limit_bytes=56 * 1024 * 1024
        ),
    )(
        embedded,
        outbox,
        loss_grad,
        grad_outbox,
        stash_held,
        norm_gain,
        w_query.reshape(tensors, width, width),
        w_keyval.reshape(tensors, width, 2 * HEAD),
        w_out[0],
    )


def solution(mesh):
    return jax.shard_map(
        local,
        mesh=mesh,
        in_specs=(
            P(None, "tensor"),
            P("section", None, "tensor"),
            P(None, "tensor"),
            P("section", None, "tensor"),
            P("section", None, "tensor"),
            P("section", "tensor"),
            P("section", None, "tensor"),
            P("section", None, "tensor"),
            P("section", "tensor", None),
        ),
        out_specs=(
            P("section", None, "tensor"),
            P("section", None, "tensor"),
            P("section", None, "tensor"),
        ),
        check_vma=False,
    )
```

time: 241 us -> 125 us (0.52)
  the two profiles are of different devices: /device:TPU:33 before, /device:TPU:18 now
where the time goes in v2:
time: 125 us
  Pallas kernels  119 us (95%)
  local copies, waits for them, and re-layouts  5.01 us (4%)
    pallas_call x1, Pallas kernels, local(): pl.pallas_call(kernel, out_shape=(shard, shard, shard), in_specs=[anywher...  119 us
    unnamed x3, local copies, waits for them, and re-layouts  5.01 us

profile of v2, /device:TPU:18, one launch (start us, length us, event | category | flops | bytes accessed | tf_op | source)
XLA Modules:
  0.0 124.9 jit_solution(7253229991555293016)
XLA Ops:
  0.6 119.3 %shard_map.112 = (bf16[1,256,512]{2,1,0:T(8,128)(2,1)}, bf16[1,256,512]{2,1,0:T(8,128)(2,1)}, bf16[1,256,512]{2,1,0:T(8,128)(2,1)}) custom-call(bf16[256,512]{1,0:T(8,128)(2,1)} %embedded.1, bf16[1,256,512]{2,1,0:T(8,128)(2,1)} %outbox.1, bf16[256,512]{1,0:T(8,128)(2,1)} %loss_grad.1, bf16[1,256,512]{2,1,0:T(8,128)(2,1)} %grad_outbox.1, ...), custom_call_target="tpu_custom_call" | custom-call | tf_op jit(solution)/shard_map/pallas_call | solution.py:532
  119.9 1.7 %copy.15 = bf16[1,256,512]{2,1,0:T(8,128)(2,1)} copy(bf16[1,256,512]{2,1,0:T(8,128)(2,1)} %get-tuple-element.6) | data formatting | bytes 524288
  121.6 1.7 %copy.16 = bf16[1,256,512]{2,1,0:T(8,128)(2,1)} copy(bf16[1,256,512]{2,1,0:T(8,128)(2,1)} %get-tuple-element.7) | data formatting | bytes 524288
  123.2 1.7 %copy.17 = bf16[1,256,512]{2,1,0:T(8,128)(2,1)} copy(bf16[1,256,512]{2,1,0:T(8,128)(2,1)} %get-tuple-element.8) | data formatting | bytes 524288

commit v3 on v2

--- a/solution.py
+++ b/solution.py
@@ -12,6 +12,7 @@
 NT = (((1,), (1,)), ((), ()))
 TN = (((0,), (0,)), ((), ()))
 STASH, GRAD, FRESH = 0, 1, 2
+PARTS = 4
 
 
 def dot(a, b, dims=(((1,), (0,)), ((), ()))):
@@ -55,6 +56,7 @@
     ring_in,
     last_in,
     result,
+    staged,
     weight_sem,
     local_sem,
     gain_send,
@@ -84,6 +86,8 @@
     features = width * tensors
     heads = width // HEAD
     halves = [pl.ds(0, half), pl.ds(half, half)]
+    quarter = seq // PARTS
+    quarters = [pl.ds(part * quarter, quarter) for part in range(PARTS)]
     parity = lax.rem(s, 2)
     chip = t // 2
     core = lax.rem(t, 2)
@@ -155,6 +159,15 @@
     for copy in weights:
         copy.start()
     gain_copy.wait()
+
+    @pl.when(final)
+    def _():
+        pltpu.make_async_copy(embedded, staged, local_sem.at[1]).start()
+
+    @pl.when(jnp.logical_not(final))
+    def _():
+        pltpu.make_async_copy(outbox.at[0], staged, local_sem.at[1]).start()
+
     gains[t] = gain_raw[...].astype(F32)
 
     @pl.when(goes_away)
@@ -165,46 +178,48 @@
     def _():
         pl.semaphore_wait(barrier, len(peers))
 
-    def near(which, src):
-        copies = []
-        for part, rows in enumerate(halves):
-            for side, tensor in enumerate((above, below)):
-                copies.append(
-                    remote(
-                        src.at[rows],
-                        full.at[which, t, rows],
-                        near_send.at[which, side, part],
-                        near_recv.at[which, side, part],
-                        targets[which],
-                        tensor,
-                    )
-                )
-        return copies
-
-    def near_start(which, usual, other, use_other):
-        if other is None:
-            for copy in near(which, usual):
-                copy.start()
-        else:
-
-            @pl.when(use_other)
-            def _():
-                for copy in near(which, other):
-                    copy.start()
-
-            @pl.when(jnp.logical_not(use_other))
-            def _():
-                for copy in near(which, usual):
-                    copy.start()
-
-        pending.extend(near(which, usual))
+    def near(which, src, parts):
+        return [
+            remote(
+                src.at[quarters[part]],
+                full.at[which, t, quarters[part]],
+                near_send.at[which, side, part],
+                near_recv.at[which, side, part],
+                targets[which],
+                tensor,
+            )
+            for part in parts
+            for side, tensor in enumerate((above, below))
+        ]
+
+    def near_start(which, src):
+        for copy in near(which, src, range(PARTS)):
+            copy.start()
+
+    def fresh_start():
+        @pl.when(final)
+        def _():
+            near_start(FRESH, embedded)
+
+        @pl.when(jnp.logical_not(final))
+        def _():
+            near_start(FRESH, outbox.at[0])
+
+    def grad_start():
+        @pl.when(s == 0)
+        def _():
+            near_start(GRAD, loss_grad)
+
+        @pl.when(s != 0)
+        def _():
+            near_start(GRAD, grad_outbox.at[0])
 
     low = lax.rem(chip + parity + chips - 1, chips)
     high = lax.rem(chip + parity, chips)
     slots = [low, high, lax.rem(low + chips - 1, chips), lax.rem(high + 1, chips)]
 
-    def pass_near(which):
-        for part, rows in enumerate(halves):
+    def pass_near(which, after=None):
+        for part, rows in enumerate(quarters):
             for side, ahead in enumerate((up, down)):
                 here = full.at[which, 2 * slots[side] + core, rows]
                 arrived(here, near_send.at[which, side, part], near_recv.at[which, side, part])
@@ -224,9 +239,11 @@
                     s,
                     sibling,
                 )
+            if after is not None:
+                after(part)
 
     def pass_far(which):
-        for part, rows in enumerate(halves):
+        for part, rows in enumerate(quarters):
             for side in range(2):
                 here = full.at[which, 2 * slots[2 + side] + core, rows]
                 arrived(here, far_send.at[which, side, part], far_recv.at[which, side, part])
@@ -240,7 +257,7 @@
                 )
 
     def gathered(which):
-        for part, rows in enumerate(halves):
+        for part, rows in enumerate(quarters):
             for place in range(4):
                 here = full.at[which, 2 * slots[place] + 1 - core, rows]
                 arrived(here, sib_send.at[which, place, part], sib_recv.at[which, place, part])
@@ -377,7 +394,17 @@
         arrived(last_in.at[which, 1, halves[1]], rs_send.at[which, 5], rs_recv.at[which, 5])
         return own[which] + last_in[which, 0].astype(F32) + last_in[which, 1].astype(F32)
 
-    near_start(STASH, stash.at[0], None, None)
+    for copy in near(STASH, stash.at[0], (0, 1)):
+        copy.start()
+
+    @pl.when(parity == 0)
+    def _():
+        fresh_start()
+
+    @pl.when(parity == 1)
+    def _():
+        grad_start()
+
     for step in range(1, tensors):
         launch(
             gains.at[t],
@@ -387,26 +414,29 @@
             s,
             lax.rem(t + step, tensors),
         )
-    near_start(GRAD, grad_outbox.at[0], loss_grad, s == 0)
-
-    evict_copy = remote(outbox.at[0], evicted.at[0], evict_send, evict_recv, mirror, t)
-
-    @pl.when(goes_away)
-    def _():
-        evict_copy.start()
-
-    @pl.when(stays)
-    def _():
-        pltpu.make_async_copy(outbox.at[0], evicted.at[0], local_sem.at[1]).start()
-
-    @pl.when(final)
-    def _():
-        pltpu.make_async_copy(embedded, evicted.at[0], local_sem.at[1]).start()
-
-    pass_near(STASH)
-    near_start(FRESH, outbox.at[0], embedded, final)
+
+    def more_stash(part):
+        for copy in near(STASH, stash.at[0], (part,)):
+            copy.wait_send()
+        if part + 2 < PARTS:
+            for copy in near(STASH, stash.at[0], (part + 2,)):
+                copy.start()
+
+    pass_near(STASH, more_stash)
+
+    @pl.when(parity == 1)
+    def _():
+        fresh_start()
+
+    @pl.when(parity == 0)
+    def _():
+        grad_start()
+
+    pending.extend(near(GRAD, grad_outbox.at[0], range(PARTS)))
+    pending.extend(near(FRESH, outbox.at[0], range(PARTS)))
     pass_far(STASH)
     pass_near(GRAD)
+    pass_near(FRESH)
     for step in range(1, tensors):
         here = gains.at[lax.rem(t + tensors - step, tensors)]
         arrived(here, gain_send.at[step], gain_recv.at[step])
@@ -416,7 +446,6 @@
     inv_back = project(STASH)
     inv_ref[...] = jnp.broadcast_to(inv_back, inv_ref.shape)
     pass_far(GRAD)
-    pass_near(FRESH)
     gathered(GRAD)
 
     acc_g[...] = jnp.zeros_like(acc_g)
@@ -464,6 +493,19 @@
         return dot(flat[...], wq[block], NT) + dot(dpair_low[...], wkv[block], NT)
 
     reduce_start(0, back_term)
+
+    pltpu.make_async_copy(outbox.at[0], staged, local_sem.at[1]).wait()
+    evict_copy = remote(staged, evicted.at[0], evict_send, evict_recv, mirror, t)
+    keep_copy = pltpu.make_async_copy(staged, evicted.at[0], local_sem.at[1])
+
+    @pl.when(goes_away)
+    def _():
+        evict_copy.start()
+
+    @pl.when(jnp.logical_not(goes_away))
+    def _():
+        keep_copy.start()
+
     pass_far(FRESH)
     gathered(FRESH)
     project(FRESH)
@@ -506,7 +548,7 @@
 
     @pl.when(jnp.logical_not(goes_away))
     def _():
-        pltpu.make_async_copy(outbox.at[0], evicted.at[0], local_sem.at[1]).wait()
+        keep_copy.wait()
 
     grad_copy.wait()
     mixed = reduce_end(1)
@@ -516,6 +558,12 @@
     for copy in pending:
         copy.wait_send()
     out_copy.wait()
+
+
+def hand_over(a, b, c, x, y, z):
+    x[...] = a[...]
+    y[...] = b[...]
+    z[...] = c[...]
 
 
 def local(
@@ -529,7 +577,7 @@
     shard = jax.ShapeDtypeStruct(outbox.shape, BF16)
     dma = pltpu.SemaphoreType.DMA
     anywhere = pl.BlockSpec(memory_space=pl.ANY)
-    return pl.pallas_call(
+    parts = pl.pallas_call(
         kernel,
         out_shape=(shard, shard, shard),
         in_specs=[anywhere] * 9,
@@ -559,18 +607,19 @@
             pltpu.VMEM((2, 2, half, width), BF16),
             pltpu.VMEM((2, 2, seq, width), BF16),
             pltpu.VMEM((2, seq, width), BF16),
+            pltpu.VMEM((seq, width), BF16),
             dma((2 + tensors,)),
             dma((4,)),
             dma((tensors,)),
             dma((tensors,)),
             dma((tensors,)),
             dma((tensors,)),
-            dma((3, 2, 2)),
-            dma((3, 2, 2)),
-            dma((3, 2, 2)),
-            dma((3, 2, 2)),
-            dma((3, 4, 2)),
-            dma((3, 4, 2)),
+            dma((3, 2, PARTS)),
+            dma((3, 2, PARTS)),
+            dma((3, 2, PARTS)),
+            dma((3, 2, PARTS)),
+            dma((3, 4, PARTS)),
+            dma((3, 4, PARTS)),
             dma,
             dma,
             dma((2, chips)),
@@ -592,6 +641,10 @@
         w_keyval.reshape(tensors, width, 2 * HEAD),
         w_out[0],
     )
+    return pl.pallas_call(
+        hand_over,
+        out_shape=(shard, shard, shard),
+    )(*parts)
 
 
 def solution(mesh):

time: 125 us -> 114 us (0.912)
  the two profiles are of different devices: /device:TPU:18 before, /device:TPU:3 now
where the time goes in v3:
time: 114 us
  Pallas kernels  113 us (99%)
    pallas_call x1, Pallas kernels, local(): pl.pallas_call(kernel, out_shape=(shard, shard, shard), in_specs=[anywher...  111 us

profile of v3, /device:TPU:3, one launch (start us, length us, event | category | flops | bytes accessed | tf_op | source)
XLA Modules:
  0.0 114.0 jit_solution(90819065152326453)
XLA Ops:
  0.6 111.4 %shard_map.112 = (bf16[1,256,512]{2,1,0:T(8,128)(2,1)}, bf16[1,256,512]{2,1,0:T(8,128)(2,1)}, bf16[1,256,512]{2,1,0:T(8,128)(2,1)}) custom-call(bf16[256,512]{1,0:T(8,128)(2,1)} %embedded.1, bf16[1,256,512]{2,1,0:T(8,128)(2,1)} %outbox.1, bf16[256,512]{1,0:T(8,128)(2,1)} %loss_grad.1, bf16[1,256,512]{2,1,0:T(8,128)(2,1)} %grad_outbox.1, ...), custom_call_target="tpu_custom_call" | custom-call | tf_op jit(solution)/shard_map/pallas_call | solution.py:580
  112.0 2.0 %shard_map.113 = (bf16[1,256,512]{2,1,0:T(8,128)(2,1)}, bf16[1,256,512]{2,1,0:T(8,128)(2,1)}, bf16[1,256,512]{2,1,0:T(8,128)(2,1)}) custom-call(bf16[1,256,512]{2,1,0:T(8,128)(2,1)} %get-tuple-element.6.a, bf16[1,256,512]{2,1,0:T(8,128)(2,1)} %get-tuple-element.7.b, bf16[1,256,512]{2,1,0:T(8,128)(2,1)} %get-tuple-element.8.c), custom_call_target="tpu_custom_call" | custom-call | tf_op jit(solution)/shard_map/pallas_call | solution.py:644

commit v4 on v3

--- a/solution.py
+++ b/solution.py
@@ -57,6 +57,7 @@
     last_in,
     result,
     staged,
+    probs,
     weight_sem,
     local_sem,
     gain_send,
@@ -256,9 +257,9 @@
                     sibling,
                 )
 
-    def gathered(which):
+    def gathered(which, places=(0, 1, 2, 3)):
         for part, rows in enumerate(quarters):
-            for place in range(4):
+            for place in places:
                 here = full.at[which, 2 * slots[place] + 1 - core, rows]
                 arrived(here, sib_send.at[which, place, part], sib_recv.at[which, place, part])
 
@@ -301,30 +302,16 @@
         return lax.rem(chip + 2 + chips - turn, chips)
 
     def reduce_start(which, term):
-        def for_sibling(turn, carry):
-            sib_out[which, turn] = term(2 * chip_at(turn) + 1 - core).astype(BF16)
-            remote(
+        def to_sibling(turn):
+            return remote(
                 sib_out.at[which, turn],
                 sib_in.at[which, turn],
                 rs_sib_send.at[which, turn],
                 rs_sib_recv.at[which, turn],
                 s,
                 sibling,
-            ).start()
-            return carry
-
-        lax.fori_loop(0, chips, for_sibling, 0)
-        for turn in range(chips):
-            pending.append(
-                remote(
-                    sib_out.at[which, turn],
-                    sib_in.at[which, turn],
-                    rs_sib_send.at[which, turn],
-                    rs_sib_recv.at[which, turn],
-                    s,
-                    sibling,
-                )
             )
+
         opening = [
             (0, 0, 0, ring_in.at[which, 0], up),
             (0, 1, 1, ring_in.at[which, 1], down),
@@ -346,28 +333,39 @@
                 if at == turn
             ]
 
-        def for_self(turn, carry):
-            mine = term(2 * chip_at(turn) + core)
-            arrived(
-                sib_in.at[which, turn], rs_sib_send.at[which, turn], rs_sib_recv.at[which, turn]
-            )
-            total = mine + sib_in[which, turn].astype(F32)
-            sums[which, turn] = total.astype(BF16)
-
-            @pl.when(turn == 2)
+        def step(stage, carry):
+            @pl.when(stage < chips)
             def _():
-                own[which] = total
-
-            for at in (0, 1, 3):
-
-                @pl.when(turn == at)
+                sib_out[which, stage] = term(2 * chip_at(stage) + 1 - core).astype(BF16)
+                to_sibling(stage).start()
+
+            @pl.when(stage > 0)
+            def _():
+                turn = stage - 1
+                mine = term(2 * chip_at(turn) + core)
+                arrived(
+                    sib_in.at[which, turn],
+                    rs_sib_send.at[which, turn],
+                    rs_sib_recv.at[which, turn],
+                )
+                total = mine + sib_in[which, turn].astype(F32)
+                sums[which, turn] = total.astype(BF16)
+
+                @pl.when(turn == 2)
                 def _():
-                    for copy in sends(at):
-                        copy.start()
+                    own[which] = total
+
+                for at in (0, 1, 3):
+
+                    @pl.when(turn == at)
+                    def _():
+                        for copy in sends(at):
+                            copy.start()
 
             return carry
 
-        lax.fori_loop(0, chips, for_self, 0)
+        lax.fori_loop(0, chips + 1, step, 0)
+        pending.extend(to_sibling(turn) for turn in range(chips))
         for at in (0, 1, 3):
             pending.extend(sends(at))
 
@@ -436,7 +434,6 @@
     pending.extend(near(FRESH, outbox.at[0], range(PARTS)))
     pass_far(STASH)
     pass_near(GRAD)
-    pass_near(FRESH)
     for step in range(1, tensors):
         here = gains.at[lax.rem(t + tensors - step, tensors)]
         arrived(here, gain_send.at[step], gain_recv.at[step])
@@ -445,22 +442,36 @@
     gathered(STASH)
     inv_back = project(STASH)
     inv_ref[...] = jnp.broadcast_to(inv_back, inv_ref.shape)
+
+    def keep_probability(head, carry):
+        probs[head] = probability(head)
+        return carry
+
+    lax.fori_loop(0, heads, keep_probability, 0)
+    acc_g[...] = jnp.zeros_like(acc_g)
+
+    def pull_back(places):
+        def step(at, carry):
+            block = 2 * slots[places[0]] + at
+            other = 2 * slots[places[1]] + at
+            acc_g[...] += dot(full[GRAD, block], wo[block], NT) + dot(
+                full[GRAD, other], wo[other], NT
+            )
+            return carry
+
+        gathered(GRAD, places)
+        lax.fori_loop(0, 2, step, 0)
+
+    pull_back((0, 1))
+    pass_near(FRESH)
     pass_far(GRAD)
-    gathered(GRAD)
-
-    acc_g[...] = jnp.zeros_like(acc_g)
-
-    def pull_back(block, carry):
-        acc_g[...] += dot(full[GRAD, block], wo[block], NT)
-        return carry
-
-    lax.fori_loop(0, tensors, pull_back, 0)
+    pull_back((2, 3))
     for head in range(heads):
         dquery_h[head] = acc_g[:, head * HEAD : (head + 1) * HEAD].astype(BF16)
     dpair[...] = jnp.zeros_like(dpair)
 
     def head_back(head, total):
-        prob = probability(head)
+        prob = probs[head]
         d_head = dquery_h[head]
         d_prob = dot(d_head, keyval[1], NT)
         d_score = prob * (d_prob - jnp.sum(prob * d_prob, axis=-1, keepdims=True))
@@ -560,10 +571,22 @@
     out_copy.wait()
 
 
-def hand_over(a, b, c, x, y, z):
-    x[...] = a[...]
-    y[...] = b[...]
-    z[...] = c[...]
+def hand_over(*refs):
+    sources, targets = refs[:3], refs[3:6]
+    staged, sems = refs[6:]
+    inward = [
+        pltpu.make_async_copy(sources[at], staged.at[at], sems.at[0, at]) for at in range(3)
+    ]
+    outward = [
+        pltpu.make_async_copy(staged.at[at], targets[at], sems.at[1, at]) for at in range(3)
+    ]
+    for copy in inward:
+        copy.start()
+    for came, goes in zip(inward, outward):
+        came.wait()
+        goes.start()
+    for copy in outward:
+        copy.wait()
 
 
 def local(
@@ -608,6 +631,7 @@
             pltpu.VMEM((2, 2, seq, width), BF16),
             pltpu.VMEM((2, seq, width), BF16),
             pltpu.VMEM((seq, width), BF16),
+            pltpu.VMEM((heads, seq, seq), F32),
             dma((2 + tensors,)),
             dma((4,)),
             dma((tensors,)),
@@ -644,6 +668,9 @@
     return pl.pallas_call(
         hand_over,
         out_shape=(shard, shard, shard),
+        in_specs=[anywhere] * 3,
+        out_specs=(anywhere, anywhere, anywhere),
+        scratch_shapes=[pltpu.VMEM((3,) + outbox.shape, BF16), dma((2, 3))],
     )(*parts)
 
 

time: 114 us -> 109 us (0.956)
  the two profiles are of different devices: /device:TPU:3 before, /device:TPU:33 now
where the time goes in v4:
time: 109 us; the launch traced here: 108 us
  Pallas kernels  108 us (99%)
    pallas_call x1, Pallas kernels, local(): pl.pallas_call(kernel, out_shape=(shard, shard, shard), in_specs=[anywher...  106 us

profile of v4, /device:TPU:33, one launch (start us, length us, event | category | flops | bytes accessed | tf_op | source)
XLA Modules:
  0.0 108.4 jit_solution(12566533741783300911)
XLA Ops:
  0.6 105.9 %shard_map.112 = (bf16[1,256,512]{2,1,0:T(8,128)(2,1)}, bf16[1,256,512]{2,1,0:T(8,128)(2,1)}, bf16[1,256,512]{2,1,0:T(8,128)(2,1)}) custom-call(bf16[256,512]{1,0:T(8,128)(2,1)} %embedded.1, bf16[1,256,512]{2,1,0:T(8,128)(2,1)} %outbox.1, bf16[256,512]{1,0:T(8,128)(2,1)} %loss_grad.1, bf16[1,256,512]{2,1,0:T(8,128)(2,1)} %grad_outbox.1, ...), custom_call_target="tpu_custom_call" | custom-call | tf_op jit(solution)/shard_map/pallas_call | solution.py:603
  106.5 1.9 %shard_map.113 = (bf16[1,256,512]{2,1,0:T(8,128)(2,1)}, bf16[1,256,512]{2,1,0:T(8,128)(2,1)}, bf16[1,256,512]{2,1,0:T(8,128)(2,1)}) custom-call(bf16[1,256,512]{2,1,0:T(8,128)(2,1)} %get-tuple-element.6.refs_0_, bf16[1,256,512]{2,1,0:T(8,128)(2,1)} %get-tuple-element.7.refs_1_, bf16[1,256,512]{2,1,0:T(8,128)(2,1)} %get-tuple-element.8.refs_2_), custom_call_target="tpu_custom_call" | custom-call | tf_op jit(solution)/shard_map/pallas_call | solution.py:668

commit v5 on v4

--- a/solution.py
+++ b/solution.py
@@ -145,32 +145,6 @@
             barrier, inc=1, device_id=(mirror, t), device_id_type=pl.DeviceIdType.MESH
         )
 
-    gain_copy = pltpu.make_async_copy(gain, gain_raw, local_sem.at[0])
-    gain_copy.start()
-    weights = [
-        pltpu.make_async_copy(w_query, wq, weight_sem.at[0]),
-        pltpu.make_async_copy(w_keyval, wkv, weight_sem.at[1]),
-    ]
-    for block in range(tensors):
-        weights.append(
-            pltpu.make_async_copy(
-                w_out.at[:, pl.ds(block * width, width)], wo.at[block], weight_sem.at[2 + block]
-            )
-        )
-    for copy in weights:
-        copy.start()
-    gain_copy.wait()
-
-    @pl.when(final)
-    def _():
-        pltpu.make_async_copy(embedded, staged, local_sem.at[1]).start()
-
-    @pl.when(jnp.logical_not(final))
-    def _():
-        pltpu.make_async_copy(outbox.at[0], staged, local_sem.at[1]).start()
-
-    gains[t] = gain_raw[...].astype(F32)
-
     @pl.when(goes_away)
     def _():
         pl.semaphore_wait(barrier, len(peers) + 1)
@@ -219,8 +193,9 @@
     high = lax.rem(chip + parity, chips)
     slots = [low, high, lax.rem(low + chips - 1, chips), lax.rem(high + 1, chips)]
 
-    def pass_near(which, after=None):
-        for part, rows in enumerate(quarters):
+    def pass_near(which, after=None, parts=range(PARTS)):
+        for part in parts:
+            rows = quarters[part]
             for side, ahead in enumerate((up, down)):
                 here = full.at[which, 2 * slots[side] + core, rows]
                 arrived(here, near_send.at[which, side, part], near_recv.at[which, side, part])
@@ -390,7 +365,7 @@
         arrived(last_in.at[which, 1, halves[0]], rs_send.at[which, 3], rs_recv.at[which, 3])
         arrived(last_in.at[which, 0, halves[0]], rs_send.at[which, 4], rs_recv.at[which, 4])
         arrived(last_in.at[which, 1, halves[1]], rs_send.at[which, 5], rs_recv.at[which, 5])
-        return own[which] + last_in[which, 0].astype(F32) + last_in[which, 1].astype(F32)
+        return last_in[which, 0].astype(F32) + last_in[which, 1].astype(F32)
 
     for copy in near(STASH, stash.at[0], (0, 1)):
         copy.start()
@@ -402,6 +377,32 @@
     @pl.when(parity == 1)
     def _():
         grad_start()
+
+    gain_copy = pltpu.make_async_copy(gain, gain_raw, local_sem.at[0])
+    gain_copy.start()
+    weights = [
+        pltpu.make_async_copy(w_query, wq, weight_sem.at[0]),
+        pltpu.make_async_copy(w_keyval, wkv, weight_sem.at[1]),
+    ]
+    for block in range(tensors):
+        weights.append(
+            pltpu.make_async_copy(
+                w_out.at[:, pl.ds(block * width, width)], wo.at[block], weight_sem.at[2 + block]
+            )
+        )
+    for copy in weights:
+        copy.start()
+    gain_copy.wait()
+
+    @pl.when(final)
+    def _():
+        pltpu.make_async_copy(embedded, staged, local_sem.at[1]).start()
+
+    @pl.when(jnp.logical_not(final))
+    def _():
+        pltpu.make_async_copy(outbox.at[0], staged, local_sem.at[1]).start()
+
+    gains[t] = gain_raw[...].astype(F32)
 
     for step in range(1, tensors):
         launch(
@@ -440,6 +441,18 @@
     for copy in weights:
         copy.wait()
     gathered(STASH)
+    pltpu.make_async_copy(outbox.at[0], staged, local_sem.at[1]).wait()
+    evict_copy = remote(staged, evicted.at[0], evict_send, evict_recv, mirror, t)
+    keep_copy = pltpu.make_async_copy(staged, evicted.at[0], local_sem.at[1])
+
+    @pl.when(goes_away)
+    def _():
+        evict_copy.start()
+
+    @pl.when(jnp.logical_not(goes_away))
+    def _():
+        keep_copy.start()
+
     inv_back = project(STASH)
     inv_ref[...] = jnp.broadcast_to(inv_back, inv_ref.shape)
 
@@ -463,8 +476,9 @@
         lax.fori_loop(0, 2, step, 0)
 
     pull_back((0, 1))
-    pass_near(FRESH)
+    pass_near(FRESH, parts=(0, 1))
     pass_far(GRAD)
+    pass_near(FRESH, parts=(2, 3))
     pull_back((2, 3))
     for head in range(heads):
         dquery_h[head] = acc_g[:, head * HEAD : (head + 1) * HEAD].astype(BF16)
@@ -505,18 +519,6 @@
 
     reduce_start(0, back_term)
 
-    pltpu.make_async_copy(outbox.at[0], staged, local_sem.at[1]).wait()
-    evict_copy = remote(staged, evicted.at[0], evict_send, evict_recv, mirror, t)
-    keep_copy = pltpu.make_async_copy(staged, evicted.at[0], local_sem.at[1])
-
-    @pl.when(goes_away)
-    def _():
-        evict_copy.start()
-
-    @pl.when(jnp.logical_not(goes_away))
-    def _():
-        keep_copy.start()
-
     pass_far(FRESH)
     gathered(FRESH)
     project(FRESH)
@@ -535,7 +537,7 @@
 
     reduce_start(1, forward_term)
 
-    summed = reduce_end(0)
+    summed = own[0] + reduce_end(0)
     for step in range(1, tensors):
         here = row_sums.at[lax.rem(t + tensors - step, tensors)]
         arrived(here, row_send.at[step], row_recv.at[step])
@@ -562,11 +564,13 @@
         keep_copy.wait()
 
     grad_copy.wait()
-    mixed = reduce_end(1)
-    result[1] = (full[FRESH, t].astype(F32) + mixed).astype(BF16)
+    for copy in pending[:-2]:
+        copy.wait_send()
+    own[1] = full[FRESH, t].astype(F32) + own[1]
+    result[1] = (own[1] + reduce_end(1)).astype(BF16)
     out_copy = pltpu.make_async_copy(result.at[1], section_out.at[0], local_sem.at[3])
     out_copy.start()
-    for copy in pending:
+    for copy in pending[-2:]:
         copy.wait_send()
     out_copy.wait()
 

time: 109 us -> 108 us (level)
    pallas_call x1, Pallas kernels: 106 us -> 105 us  [local(): pl.pallas_call(kernel, out_shape=(shard, shard, shard), in_specs=[anywher...]
where the time goes in v5:
time: 108 us; the launch traced here: 107 us
  Pallas kernels  107 us (99%)
    pallas_call x1, Pallas kernels, local(): pl.pallas_call(kernel, out_shape=(shard, shard, shard), in_specs=[anywher...  105 us

profile of v5, /device:TPU:33, one launch (start us, length us, event | category | flops | bytes accessed | tf_op | source)
XLA Modules:
  0.0 107.2 jit_solution(8392018417751975459)
XLA Ops:
  0.6 104.7 %shard_map.112 = (bf16[1,256,512]{2,1,0:T(8,128)(2,1)}, bf16[1,256,512]{2,1,0:T(8,128)(2,1)}, bf16[1,256,512]{2,1,0:T(8,128)(2,1)}) custom-call(bf16[256,512]{1,0:T(8,128)(2,1)} %embedded.1, bf16[1,256,512]{2,1,0:T(8,128)(2,1)} %outbox.1, bf16[256,512]{1,0:T(8,128)(2,1)} %loss_grad.1, bf16[1,256,512]{2,1,0:T(8,128)(2,1)} %grad_outbox.1, ...), custom_call_target="tpu_custom_call" | custom-call | tf_op jit(solution)/shard_map/pallas_call | solution.py:607
  105.3 1.9 %shard_map.113 = (bf16[1,256,512]{2,1,0:T(8,128)(2,1)}, bf16[1,256,512]{2,1,0:T(8,128)(2,1)}, bf16[1,256,512]{2,1,0:T(8,128)(2,1)}) custom-call(bf16[1,256,512]{2,1,0:T(8,128)(2,1)} %get-tuple-element.6.refs_0_, bf16[1,256,512]{2,1,0:T(8,128)(2,1)} %get-tuple-element.7.refs_1_, bf16[1,256,512]{2,1,0:T(8,128)(2,1)} %get-tuple-element.8.refs_2_), custom_call_target="tpu_custom_call" | custom-call | tf_op jit(solution)/shard_map/pallas_call | solution.py:672

commit v6 on v5

--- a/solution.py
+++ b/solution.py
@@ -330,7 +330,7 @@
                 def _():
                     own[which] = total
 
-                for at in (0, 1, 3):
+                for at in (0, 1, 3) if which == 0 else (0,):
 
                     @pl.when(turn == at)
                     def _():
@@ -341,8 +341,10 @@
 
         lax.fori_loop(0, chips + 1, step, 0)
         pending.extend(to_sibling(turn) for turn in range(chips))
-        for at in (0, 1, 3):
-            pending.extend(sends(at))
+        if which == 0:
+            for at in (0, 1, 3):
+                pending.extend(sends(at))
+        return sends(0), sends(1) + sends(3)
 
     def reduce_middle(which):
         for side, (turn, part, ahead) in enumerate(((1, 0, up), (3, 1, down))):
@@ -535,7 +537,7 @@
     def forward_term(block):
         return dot(flat[...], wo[block])
 
-    reduce_start(1, forward_term)
+    opposite, nearest = reduce_start(1, forward_term)
 
     summed = own[0] + reduce_end(0)
     for step in range(1, tensors):
@@ -553,6 +555,11 @@
     ).astype(BF16)
     grad_copy = pltpu.make_async_copy(result.at[0], input_grad.at[0], local_sem.at[2])
     grad_copy.start()
+    for copy in opposite:
+        copy.wait_send()
+    for copy in nearest:
+        copy.start()
+    pending.extend(nearest)
     reduce_middle(1)
 
     @pl.when(goes_away)

time: 108 us -> 109 us (level)
  no operation moved by 1% of the time
where the time goes in v6:
time: 109 us; the launch traced here: 108 us
  Pallas kernels  107 us (98%)
    pallas_call x1, Pallas kernels, local(): pl.pallas_call(kernel, out_shape=(shard, shard, shard), in_specs=[anywher...  105 us

profile of v6, /device:TPU:33, one launch (start us, length us, event | category | flops | bytes accessed | tf_op | source)
XLA Modules:
  0.0 107.8 jit_solution(4257706630043469659)
XLA Ops:
  0.6 105.3 %shard_map.112 = (bf16[1,256,512]{2,1,0:T(8,128)(2,1)}, bf16[1,256,512]{2,1,0:T(8,128)(2,1)}, bf16[1,256,512]{2,1,0:T(8,128)(2,1)}) custom-call(bf16[256,512]{1,0:T(8,128)(2,1)} %embedded.1, bf16[1,256,512]{2,1,0:T(8,128)(2,1)} %outbox.1, bf16[256,512]{1,0:T(8,128)(2,1)} %loss_grad.1, bf16[1,256,512]{2,1,0:T(8,128)(2,1)} %grad_outbox.1, ...), custom_call_target="tpu_custom_call" | custom-call | tf_op jit(solution)/shard_map/pallas_call | solution.py:614
  105.9 1.9 %shard_map.113 = (bf16[1,256,512]{2,1,0:T(8,128)(2,1)}, bf16[1,256,512]{2,1,0:T(8,128)(2,1)}, bf16[1,256,512]{2,1,0:T(8,128)(2,1)}) custom-call(bf16[1,256,512]{2,1,0:T(8,128)(2,1)} %get-tuple-element.6.refs_0_, bf16[1,256,512]{2,1,0:T(8,128)(2,1)} %get-tuple-element.7.refs_1_, bf16[1,256,512]{2,1,0:T(8,128)(2,1)} %get-tuple-element.8.refs_2_), custom_call_target="tpu_custom_call" | custom-call | tf_op jit(solution)/shard_map/pallas_call | solution.py:679
